TPU v7x, 32 devices: a whole 2x2x4 slice. The times are simulated.
32 devices in a mesh: grid: 4 (over z), band: 4 (over y, x), atom: 2 (over core).
Axes of the slice: x: 2, y: 2, z: 4, core: 2. Of those that a mesh axis runs over, the one named last changes fastest.
Arguments:
- psi: float32 [256, 64, 1024], P('band', 'grid'), may hold values from -27 to 27
- potential: float32 [64, 1024], P(('grid', 'atom')), may hold values from -12 to 12
- projectors: float32 [128, 4, 512], P('grid'), may hold values from -5 to 5
- strength: float32 [128, 4], P('grid'), may hold values from 0.5 to 8
- sphere_index: int32 [128, 512], P('grid'), may hold values from 2048 to 25599, as said below
- atom_count: int32 [4], P('grid'), may hold values from 2 to 32, as said below
Outputs:
- orthonormal: float32 [256, 64, 1024], P('band', ('grid', 'atom'))
Inputs may be any that keep to these rules, and one draw needn't show every extreme that they name: `sphere_index`: row a lists the 512 cells of an 8 x 8 x 8 cube about the atom's centre, offsets -4 to 3 in each direction, as e * 1024 + x * 32 + y with e counted from 6 rows below its domain. `atom_count`: the live slots of a domain are its first ones; in every draw some domain has all 32 live.
All inputs are finite; a program needn't handle non-finite values.
Results may differ from a plain program's by a relative error of at most 0.0003.
Values sent between devices are 32-bit elements; how exact they have to be, the bound alone decides.
A program may use at most 128 MiB of HBM per device.

v0:
```python
import math

import jax
import jax.numpy as jnp
from jax import lax
from jax.sharding import PartitionSpec as P

BANDS = 256
CY = 32


STENCIL = (
    -5369.0 / 1800.0,
    12.0 / 7.0,
    -15.0 / 56.0,
    10.0 / 189.0,
    -1.0 / 112.0,
    2.0 / 1925.0,
    -1.0 / 16632.0,
)
KINETIC = -0.5 * 4.0
STEP_SIZE = 0.05
HIGHEST = lax.Precision.HIGHEST


def from_behind(block, axis, distance):
    devices = range(lax.axis_size(axis))
    route = [((i - distance) % len(devices), i) for i in devices]
    return lax.ppermute(block, axis, route)


def extended_2(x, sides, width):
    for axis, dim in sides:
        count, length = (lax.axis_size(axis), x.shape[dim])
        up = [(i, (i + 1) % count) for i in range(count)]
        down = [(j, i) for i, j in up]
        last = lax.slice_in_dim(x, length - width, length, axis=dim)
        first = lax.slice_in_dim(x, 0, width, axis=dim)
        before = lax.ppermute(last, axis, up)
        after = lax.ppermute(first, axis, down)
        x = jnp.concatenate([before, x, after], axis=dim)
    return x


def inner_rows(left, right):
    return lax.dot_general(
        left, right, (((1,), (1,)), ((), ())), precision=HIGHEST, preferred_element_type=jnp.float32
    )


def spread_terms(weighted, projectors, sphere_index, total_cells):
    band_rows = weighted.shape[0]
    values = jnp.einsum("nai,ais->nas", weighted, projectors, precision=HIGHEST)
    dense = jnp.zeros((band_rows, total_cells), jnp.float32)
    return dense.at[:, sphere_index.reshape(-1)].add(values.reshape(band_rows, -1))


def fold_rims(dense, depth):
    from_below = from_behind(dense[:, depth + 6 :], "grid", 1)
    from_above = from_behind(dense[:, :6], "grid", -1)
    inner = dense[:, 6 : depth + 6]
    inner = inner.at[:, :6].add(from_below)
    return inner.at[:, depth - 6 :].add(from_above)


def body(psi, potential, projectors, strength, sphere_index, atom_count):
    band_rows, depth, plane_cells = psi.shape
    groups = lax.axis_size("atom")
    core = lax.axis_index("atom")
    half = depth // groups
    extended = extended_2(psi, (("grid", 1),), 6)
    window = lax.dynamic_slice_in_dim(extended, core * half, half + 12, 1)
    centre = window[:, 6 : 6 + half]
    margin = 6 * CY
    padded = jnp.pad(centre, ((0, 0), (0, 0), (margin, margin)))
    column = lax.iota(jnp.int32, plane_cells) % CY
    laplace = 3.0 * STENCIL[0] * centre
    for k in range(1, 7):
        along_z = window[:, 6 + k : 6 + k + half] + window[:, 6 - k : 6 - k + half]
        along_x = (
            padded[:, :, margin + k * CY : margin + k * CY + plane_cells]
            + padded[:, :, margin - k * CY : margin - k * CY + plane_cells]
        )
        upper = jnp.where(column + k < CY, padded[:, :, margin + k : margin + k + plane_cells], 0.0)
        lower = jnp.where(column >= k, padded[:, :, margin - k : margin - k + plane_cells], 0.0)
        laplace = laplace + STENCIL[k] * (along_z + along_x + upper + lower)
    atom_slots = sphere_index.shape[0]
    share = atom_slots // groups
    alive_mask = (lax.iota(jnp.int32, atom_slots) < atom_count[0]).astype(jnp.float32)
    scaled = strength * alive_mask[:, None]
    flattened = extended.reshape(band_rows, -1)
    total_cells = flattened.shape[1]
    own_index = lax.dynamic_slice_in_dim(sphere_index, core * share, share, 0)
    own_projectors = lax.dynamic_slice_in_dim(projectors, core * share, share, 0)
    own_scaled = lax.dynamic_slice_in_dim(scaled, core * share, share, 0)
    points = flattened[:, own_index]
    intersections = jnp.einsum(
        "nas,ais->nai", points, own_projectors, precision=HIGHEST
    ) / math.sqrt(projectors.shape[2])
    weighted = intersections * own_scaled[None]
    dense = spread_terms(weighted, own_projectors, own_index, total_cells).reshape(
        band_rows, depth + 12, plane_cells
    )
    nonlocal_half = lax.psum_scatter(
        fold_rims(dense, depth), "atom", scatter_dimension=1, tiled=True
    )
    updated = centre - STEP_SIZE * (KINETIC * laplace + potential * centre + nonlocal_half)
    flat_rows = updated.reshape(band_rows, half * plane_cells)
    cells_total = lax.axis_size("grid") * depth * plane_cells
    block = inner_rows(flat_rows, lax.all_gather(flat_rows, "band", axis=0, tiled=True))
    summed_rows = lax.psum(block, ("grid", "atom")) / cells_total
    intersection_matrix = lax.all_gather(summed_rows, "band", axis=0, tiled=True)
    factor = jnp.linalg.cholesky(intersection_matrix)
    inverse = lax.linalg.triangular_solve(
        factor, jnp.eye(BANDS, dtype=jnp.float32), left_side=True, lower=True
    )
    own_inverse = lax.dynamic_slice_in_dim(
        inverse, lax.axis_index("band") * band_rows, band_rows, 0
    )
    result = jnp.dot(
        own_inverse,
        lax.all_gather(flat_rows, "band", axis=0, tiled=True),
        precision=HIGHEST,
        preferred_element_type=jnp.float32,
    )
    return result.reshape(band_rows, half, plane_cells)


def solution(mesh):
    in_specs = (
        P("band", "grid", None),
        P(("grid", "atom"), None),
        P("grid", None, None),
        P("grid", None),
        P("grid", None),
        P("grid"),
    )
    out_specs = P("band", ("grid", "atom"), None)
    return jax.shard_map(body, mesh=mesh, in_specs=in_specs, out_specs=out_specs, check_vma=False)
```

profile of v0, /device:TPU:0, one launch (start us, length us, event | category | flops | bytes accessed | tf_op | source)
XLA Modules:
  0.0 547.4 jit_solution(13201074883905596832)
XLA Ops:
  6.5 2.7 fusion.95
  9.3 0.9 copy.62
  10.2 3.1 collective-permute-start
  13.3 0.9 copy.63
  14.2 2.4 collective-permute-start.1
  17.6 33.1 %collective-permute-done = f32[64,6,1024]{2,0,1:T(8,128)} collective-permute-done((f32[64,6,1024]{2,0,1:T(8,128)S(1)}, f32[64,6,1024]{2,0,1:T(8,128)}, u32[]{:S(2)}, u32[]{:S(2)}) %collective-permute-start) | collective-permute-done | bytes 1572896 | tf_op jit(solution)/shard_map/ppermute | solution.py:39
  50.7 2.7 constant_dynamic-update-slice_fusion.2
  53.5 6.6 %constant_dynamic-update-slice_fusion.1 = f32[64,28,1024]{2,0,1:T(8,128)} fusion(f32[64,28,1024]{2,0,1:T(8,128)} %constant_dynamic-update-slice_fusion.2, f32[64,16,1024]{2,1,0:T(8,128)} %param.10), kind=kLoop, calls=%fused_computation.132 | loop fusion | bytes 8388608
  60.1 23.5 %collective-permute-done.1 = f32[64,6,1024]{2,0,1:T(8,128)} collective-permute-done((f32[64,6,1024]{2,0,1:T(8,128)S(1)}, f32[64,6,1024]{2,0,1:T(8,128)}, u32[]{:S(2)}, u32[]{:S(2)}) %collective-permute-start.1) | collective-permute-done | bytes 1572896 | tf_op jit(solution)/shard_map/ppermute | solution.py:40
  83.5 2.8 constant_dynamic-update-slice_fusion
  86.4 11.1 %copy.41 = f32[64,28,1024]{0,2,1:T(8,128)} copy(f32[64,28,1024]{2,0,1:T(8,128)} %constant_dynamic-update-slice_fusion) | data formatting | bytes 14680064 | tf_op jit(solution)/shard_map/concatenate | solution.py:41
  97.5 32.9 %gather_fusion = f32[8192,64]{1,0:T(8,128)} fusion(f32[64,28672]{0,1:T(8,128)} %bitcast.71, s32[8192]{0:T(1024)S(1)} %broadcast_clamp_fusion), kind=kCustom, calls=%fused_computation | custom fusion | bytes 4227072 | tf_op jit(solution)/shard_map/gather | solution.py:96
  130.4 2.8 copy.42
  133.2 1.8 fusion.62
  135.1 1.9 convolution_bitcast_fusion
  137.2 2.7 copy.45
  139.9 50.9 %scatter_custom_fusion = f32[64,28672]{0,1:T(8,128)} fusion(s32[8192]{0:T(1024)S(1)} %bitcast.79, f32[8192,64]{1,0:T(8,128)} %copy.45, f32[]{:T(128)} %constant.181.clone.1), kind=kCustom, calls=%fused_computation.28 | custom fusion | flops 524288 | bytes 7340544 | tf_op jit(solution)/shard_map/scatter-add | solution.py:55
  190.8 7.1 %fusion.94 = (f32[64,6,1024]{0,2,1:T(8,128)}, f32[64,6,1024]{0,2,1:T(8,128)}, f32[64,6,1024]{0,2,1:T(8,128)S(1)}) fusion(f32[64,28,1024]{0,2,1:T(8,128)} %bitcast.69), kind=kLoop, calls=%fused_computation.166 | loop fusion | bytes 9437184 | tf_op jit(solution)/shard_map/slice | solution.py:60
  197.8 3.2 copy.54
  201.6 3.2 copy.55
  204.9 10.5 %collective-permute-start.3 = (f32[64,6,1024]{2,0,1:T(8,128)}, f32[64,6,1024]{2,0,1:T(8,128)}, u32[]{:S(2)}, u32[]{:S(2)}) collective-permute-start(f32[64,6,1024]{2,0,1:T(8,128)} %copy.55), channel_id=1, source_target_pairs={{8,0},{16,8},{24,16},{0,24},{9,1},{17,9},{25,17},{1,25},{10,2},{18... | collective-permute-start | bytes 4718600 | tf_op jit(solution)/shard_map/ppermute | solution.py:29
  215.4 7.5 %slice.277 = f32[64,16,1024]{0,2,1:T(8,128)} slice(f32[64,28,1024]{0,2,1:T(8,128)} %bitcast.70), slice={[0:64], [6:22], [0:1024]} | slice | bytes 8388608 | tf_op jit(solution)/shard_map/slice | solution.py:61
  222.8 2.0 copy.53
  224.9 6.9 %copy.52 = f32[64,16,1024]{2,0,1:T(8,128)} copy(f32[64,16,1024]{0,2,1:T(8,128)} %slice.277) | data formatting | bytes 8388608
  231.8 16.0 %collective-permute-done.2 = f32[64,6,1024]{2,0,1:T(8,128)} collective-permute-done((f32[64,6,1024]{2,0,1:T(8,128)}, f32[64,6,1024]{2,0,1:T(8,128)}, u32[]{:S(2)}, u32[]{:S(2)}) %collective-permute-start.2) | collective-permute-done | bytes 1572896 | tf_op jit(solution)/shard_map/ppermute | solution.py:29
  247.7 2.8 add_dynamic-update-slice_fusion
  250.6 22.7 %collective-permute-done.3 = f32[64,6,1024]{2,0,1:T(8,128)} collective-permute-done((f32[64,6,1024]{2,0,1:T(8,128)}, f32[64,6,1024]{2,0,1:T(8,128)}, u32[]{:S(2)}, u32[]{:S(2)}) %collective-permute-start.3) | collective-permute-done | bytes 1572896 | tf_op jit(solution)/shard_map/ppermute | solution.py:29
  273.2 3.4 fusion.58
  276.8 1.7 constant_dynamic-slice_fusion.1
  278.5 8.5 %reduce-scatter.2.cloned.1.call-done = f32[64,8,1024]{2,0,1:T(8,128)} async-done(((f32[64,16,1024]{2,0,1:T(8,128)}), f32[64,8,1024]{2,0,1:T(8,128)}) %reduce-scatter.2.cloned.1.call-update) | async-done | bytes 2097168 | tf_op jit(solution)/shard_map/reduce_scatter | solution.py:104
  287.1 15.7 %fusion.57 = f32[8,8,8,1024]{3,2,1,0:T(8,128)S(1)} fusion(f32[64,8,1024]{2,0,1:T(8,128)S(1)} %constant_dynamic-slice_fusion.1, f32[64,8,1024]{2,0,1:T(8,128)} %reduce-scatter.2.cloned.1.call-done, f32[64,28,1024]{2,0,1:T(8,128)} %constant_dynamic-update-slice_fusion, s32[]{:T(128)S(6)} %select_n.94, s32[]{:T(128)S(6)} %add.301, s32[]{:T(128)S(6)} %add.300, ...), kind=kLoop, calls=%fused_computation.91 | loop fusion | flops 31981568 | bytes 31502384
  302.8 1.6 copy.57
  304.5 88.8 %all-gather.2.cloned.1.call-done = f32[256,8192]{1,0:T(8,128)} async-done(((f32[64,8192]{1,0:T(8,128)}), f32[256,8192]{1,0:T(8,128)}) %all-gather.2.cloned.1.call-update) | async-done | bytes 8388624 | tf_op jit(solution)/shard_map/all_gather | solution.py:110
  393.3 10.7 %fusion.96 = f32[64,256]{1,0:T(8,128)} fusion(f32[64,8192]{1,0:T(8,128)S(1)} %bitcast.73, f32[256,8192]{1,0:T(8,128)} %all-gather.2.cloned.1.call-done), kind=kOutput, calls=%fused_computation.168 | convolution fusion | flops 1610612736 | bytes 10551296 | tf_op jit(solution)/shard_map/dot_general | solution.py:46
  404.1 54.8 %all-reduce.4.cloned.1.call-done = f32[64,256]{1,0:T(8,128)} async-done(((f32[64,256]{1,0:T(8,128)}), f32[64,256]{1,0:T(8,128)}) %all-reduce.4.cloned.1.call-update) | async-done | bytes 65552 | tf_op jit(solution)/shard_map/psum | solution.py:111
  458.9 0.8 broadcast_multiply_fusion
  459.7 9.4 %all_gather.8 = f32[256,256]{1,0:T(8,128)S(1)} all-gather(f32[64,256]{1,0:T(8,128)S(1)} %broadcast_multiply_fusion), channel_id=1, replica_groups=mesh['grid'=4,'band'=4,'atom'=2] {'band'}, dimensions={0}, use_global_device_ids=true | all-gather | bytes 327680 | tf_op jit(solution)/shard_map/all_gather | solution.py:112
  469.4 11.7 %cholesky.50 = f32[128,128]{1,0:T(8,128)S(1)} custom-call(f32[128,128]{1,0:T(8,128)S(1)} %cholesky.118), custom_call_target="Cholesky" | custom-call | tf_op jit(solution)/shard_map/jit(cholesky)/cholesky | solution.py:113
  481.2 9.8 %custom-call.14 = f32[1,128,128]{1,2,0:T(8,128)S(1)} custom-call(f32[1,128,128]{2,1,0:T(8,128)S(1)} %get-tuple-element.55), custom_call_target="InvertDiagBlocksLowerTriangular" | custom-call | tf_op jit(solution)/shard_map/jit(cholesky)/cholesky | solution.py:113
  491.4 11.7 %cholesky.105 = f32[128,128]{1,0:T(8,128)S(1)} custom-call(f32[128,128]{1,0:T(8,128)S(1)} %convolution_subtract_fusion.1), custom_call_target="Cholesky" | custom-call | tf_op jit(solution)/shard_map/jit(cholesky)/cholesky | solution.py:113
  503.2 0.7 compare_reduce_fusion
  503.9 0.6 compare_reduce_fusion.1
  505.9 4.1 while.3
  506.7 1.4 bitcast_dynamic-update-slice_fusion.2
  508.7 1.4 bitcast_dynamic-update-slice_fusion.2
  510.1 19.7 %custom-call.15 = f32[2,128,128]{1,2,0:T(8,128)S(1)} custom-call(f32[2,128,128]{2,1,0:T(8,128)S(1)} %get-tuple-element.36), custom_call_target="InvertDiagBlocksLowerTriangular" | custom-call | tf_op jit(solution)/shard_map/triangular_solve | solution.py:114
  530.6 7.5 %fusion.71 = f32[64,8192]{1,0:T(8,128)S(1)} fusion(f32[256,8192]{1,0:T(8,128)} %all-gather.2.cloned.1.call-done, s32[]{:T(128)S(6)} %select_n.112, f32[128,256]{1,0:T(8,128)S(1)} %fusion.66, f32[128,256]{1,0:T(8,128)S(1)} %fusion.74), kind=kOutput, calls=%fused_computation.114 | convolution fusion | flops 1610629120 | bytes 10747908 | tf_op jit(solution)/shard_map/dot_general | solution.py:120
  538.1 2.5 copy.60
  (57 shorter events, 4.1 us)
Async XLA Ops:
  6.5 126.7 %copy-start = (f32[32,4,512]{2,1,0:T(4,128)S(1)}, f32[32,4,512]{2,1,0:T(4,128)}, u32[]{:S(2)}) copy-start(f32[32,4,512]{2,1,0:T(4,128)} %param.12) | copy-start | bytes 786436
  6.5 280.5 %reduce-scatter.2.cloned.1.call-start = ((), (), s32[]{:S(2)}) async-start(), calls=%async_computation.1 | async-start | bytes 6291456 | tf_op jit(solution)/shard_map/reduce_scatter | solution.py:104
  10.2 6.4 %copy-start.5 = (s32[32,512]{1,0:T(8,128)S(1)}, s32[32,512]{1,0:T(8,128)}, u32[]{:S(2)}) copy-start(s32[32,512]{1,0:T(8,128)} %param.14) | copy-start | bytes 196612
  10.2 7.2 %copy-start.6 = (f32[32,4]{0,1:T(4,128)S(1)}, f32[32,4]{0,1:T(4,128)}, u32[]{:S(2)}) copy-start(f32[32,4]{0,1:T(4,128)} %param.13) | copy-start | bytes 1540
  10.2 40.5 %collective-permute-start = (f32[64,6,1024]{2,0,1:T(8,128)S(1)}, f32[64,6,1024]{2,0,1:T(8,128)}, u32[]{:S(2)}, u32[]{:S(2)}) collective-permute-start(f32[64,6,1024]{2,0,1:T(8,128)S(1)} %copy.62), channel_id=1, source_target_pairs={{0,8},{8,16},{16,24},{24,0},{1,9},{9,17},{17,25},{25,1},{2,10},{10... | collective-permute-start | bytes 4718600 | tf_op jit(solution)/shard_map/ppermute | solution.py:39
  14.2 69.3 %collective-permute-start.1 = (f32[64,6,1024]{2,0,1:T(8,128)S(1)}, f32[64,6,1024]{2,0,1:T(8,128)}, u32[]{:S(2)}, u32[]{:S(2)}) collective-permute-start(f32[64,6,1024]{2,0,1:T(8,128)S(1)} %copy.63), channel_id=1, source_target_pairs={{8,0},{16,8},{24,16},{0,24},{9,1},{17,9},{25,17},{1,25},{10,2},{18... | collective-permute-start | bytes 4718600 | tf_op jit(solution)/shard_map/ppermute | solution.py:40
  201.1 46.6 %collective-permute-start.2 = (f32[64,6,1024]{2,0,1:T(8,128)}, f32[64,6,1024]{2,0,1:T(8,128)}, u32[]{:S(2)}, u32[]{:S(2)}) collective-permute-start(f32[64,6,1024]{2,0,1:T(8,128)} %copy.54), channel_id=1, source_target_pairs={{24,0},{0,8},{8,16},{16,24},{25,1},{1,9},{9,17},{17,25},{26,2},{2,... | collective-permute-start | bytes 4718600 | tf_op jit(solution)/shard_map/ppermute | solution.py:29
  204.9 68.4 %collective-permute-start.3 = (f32[64,6,1024]{2,0,1:T(8,128)}, f32[64,6,1024]{2,0,1:T(8,128)}, u32[]{:S(2)}, u32[]{:S(2)}) collective-permute-start(f32[64,6,1024]{2,0,1:T(8,128)} %copy.55), channel_id=1, source_target_pairs={{8,0},{16,8},{24,16},{0,24},{9,1},{17,9},{25,17},{1,25},{10,2},{18... | collective-permute-start | bytes 4718600 | tf_op jit(solution)/shard_map/ppermute | solution.py:29
  224.9 22.9 %copy-start.3 = (f32[64,6,1024]{2,0,1:T(8,128)S(1)}, f32[64,6,1024]{2,0,1:T(8,128)}, u32[]{:S(2)}) copy-start(f32[64,6,1024]{2,0,1:T(8,128)} %copy.53) | copy-start | bytes 4718596
  276.7 116.6 %all-gather.2.cloned.1.call-start = ((), (), s32[]{:S(2)}) async-start(), calls=%async_computation.2 | async-start | bytes 10485760 | tf_op jit(solution)/shard_map/all_gather | solution.py:110
  276.8 10.3 %copy-start.4 = (f32[8,1024]{1,0:T(8,128)S(1)}, f32[8,1024]{1,0:T(8,128)}, u32[]{:S(2)}) copy-start(f32[8,1024]{1,0:T(8,128)} %param.11) | copy-start | bytes 98308
  304.3 89.0 %copy-start.2 = (f32[8,8,8,1024]{3,2,0,1:T(8,128)S(1)}, f32[8,8,8,1024]{3,2,0,1:T(8,128)}, u32[]{:S(2)}) copy-start(f32[8,8,8,1024]{3,2,0,1:T(8,128)} %copy.57) | copy-start | bytes 6291460
  304.4 154.5 %all-reduce.4.cloned.1.call-start = ((), (), s32[]{:S(2)}) async-start(), calls=%async_computation.3 | async-start | bytes 131072 | tf_op jit(solution)/shard_map/psum | solution.py:111
  538.1 2.5 copy-start.1
Sparse Core Ops, SparseCore 0:
  276.8 10.2 reduce-scatter.1
  304.5 88.7 all-gather.1
  404.2 54.6 all-reduce.3
where the time goes:
time: 551 us; the launch traced here: 547 us
  waiting for transfers between devices  247 us (45%)
  other arithmetic  128 us (23%)
  local copies, waits for them, and re-layouts  107 us (19%)
  matrix products  23.2 us (4%)
  starting transfers between devices  16.7 us (3%)
  between operations  15.6 us (3%)
  blocking collectives  9.45 us (2%)
    all_gather x1, waiting for transfers between devices, body(): lax.all_gather(flat_rows, 'band', axis=0, tiled=True)  88.8 us
    psum x1, waiting for transfers between devices, body(): summed_rows = lax.psum(block, ('grid', 'atom')) / cells_total  54.8 us
    scatter-add x1, other arithmetic, spread_terms(): dense.at[:, sphere_index.reshape(-1)].add(values.reshape(band_rows, -1))  50.9 us
    ppermute x2, waiting for transfers between devices, from_behind(): return lax.ppermute(block, axis, route)  38.6 us
    gather x2, local copies, waits for them, and re-layouts, body(): points = flattened[:, own_index]  35.8 us
    another operation x7, other arithmetic, body(): factor = jnp.linalg.cholesky(intersection_matrix)  34.6 us
    ppermute x1, waiting for transfers between devices, extended_2(): before = lax.ppermute(last, axis, up)  33.1 us
    unnamed x25, local copies, waits for them, and re-layouts  29.1 us
  transfers between devices with their start and end apart: 7, of which 7 were waited for; matrix products, arithmetic and copies ran while one was open for 6% of the time, Pallas kernels for 0%

commit v1 on v0

--- a/solution.py
+++ b/solution.py
@@ -1,11 +1,13 @@
+import functools
 import math
 
 import jax
 import jax.numpy as jnp
 from jax import lax
+from jax.experimental import pallas as pl
+from jax.experimental.pallas import tpu as pltpu
 from jax.sharding import PartitionSpec as P
 
-BANDS = 256
 CY = 32
 
 
@@ -21,6 +23,267 @@
 KINETIC = -0.5 * 4.0
 STEP_SIZE = 0.05
 HIGHEST = lax.Precision.HIGHEST
+MESH = pl.DeviceIdType.MESH
+
+
+def split(x):
+    hi = x.astype(jnp.bfloat16)
+    return hi, (x - hi.astype(jnp.float32)).astype(jnp.bfloat16)
+
+
+def mm(a, b, dims=((1,), (0,))):
+    return lax.dot_general(a, b, (dims, ((), ())), preferred_element_type=jnp.float32)
+
+
+def mm3(a, b, dims=((1,), (0,))):
+    ah, al = split(a)
+    bh, bl = split(b)
+    return mm(ah, bh, dims) + (mm(ah, bl, dims) + mm(al, bh, dims))
+
+
+def device(grid, band, atom):
+    return {"grid": grid, "band": band, "atom": atom}
+
+
+def gram_kernel(
+    grids, bands, atoms, scale, y_ref, yq_ref, s_ref, part, inbox, zbox, mine, a_sem, p_sem, z_sem, g_sem
+):
+    g, b, c = lax.axis_index("grid"), lax.axis_index("band"), lax.axis_index("atom")
+    plane = bands * atoms
+    me = b * atoms + c
+    rows, nb = y_ref.shape[1], y_ref.shape[2]
+    size = s_ref.shape[0]
+    depth = size // plane
+
+    def plane_peer(k):
+        p = lax.rem(me + k, plane)
+        return p, device(g, p // atoms, lax.rem(p, atoms))
+
+    barrier = pltpu.get_barrier_semaphore()
+    for k in range(1, plane):
+        pl.semaphore_signal(barrier, inc=1, device_id=plane_peer(k)[1], device_id_type=MESH)
+    for k in range(1, grids):
+        pl.semaphore_signal(
+            barrier, inc=1, device_id=device(lax.rem(g + k, grids), b, c), device_id_type=MESH
+        )
+    pl.semaphore_wait(barrier, plane - 1 + grids - 1)
+
+    own = pl.ds(pl.multiple_of(b * nb, nb), nb)
+    copies = []
+    for k in sorted(range(1, bands), key=lambda v: -v):
+        p = lax.rem(b + k, bands)
+        copies.append(
+            pltpu.make_async_remote_copy(
+                src_ref=y_ref.at[p],
+                dst_ref=yq_ref.at[:, own, :],
+                send_sem=a_sem.at[0, k - 1],
+                recv_sem=a_sem.at[1, k - 1],
+                device_id=device(g, p, c),
+                device_id_type=MESH,
+            )
+        )
+        copies[-1].start()
+    yq_ref[:, own, :] = y_ref[b]
+    for copy in copies:
+        copy.wait()
+
+    s_ref[...] = jnp.zeros_like(s_ref)
+
+    def add(r, carry):
+        hi, lo = split(yq_ref[r])
+        cross = mm(hi, lo, ((1,), (1,)))
+        s_ref[...] += mm(hi, hi, ((1,), (1,))) + (cross + cross.T)
+        return carry
+
+    lax.fori_loop(0, rows, add, 0)
+    part[...] = (s_ref[...] * scale).reshape(plane, depth, size)
+
+    copies = []
+    for k in range(1, plane):
+        p, where = plane_peer(k)
+        copies.append(
+            pltpu.make_async_remote_copy(
+                src_ref=part.at[p],
+                dst_ref=inbox.at[k - 1],
+                send_sem=p_sem.at[0, k - 1],
+                recv_sem=p_sem.at[1, k - 1],
+                device_id=where,
+                device_id_type=MESH,
+            )
+        )
+        copies[-1].start()
+    for copy in copies:
+        copy.wait()
+    total = part[me]
+    for k in range(1, plane):
+        total = total + inbox[k - 1]
+    mine[...] = total
+    zbox[g] = total
+    copies = []
+    for k in range(1, grids):
+        copies.append(
+            pltpu.make_async_remote_copy(
+                src_ref=mine,
+                dst_ref=zbox.at[g],
+                send_sem=z_sem.at[0, k - 1],
+                recv_sem=z_sem.at[1, k - 1],
+                device_id=device(lax.rem(g + k, grids), b, c),
+                device_id_type=MESH,
+            )
+        )
+        copies[-1].start()
+    for copy in copies:
+        copy.wait()
+    total = zbox[0]
+    for k in range(1, grids):
+        total = total + zbox[k]
+    piece = pl.ds(pl.multiple_of(me * depth, depth), depth)
+    mine[...] = total
+    copies = []
+    for k in range(1, plane):
+        copies.append(
+            pltpu.make_async_remote_copy(
+                src_ref=mine,
+                dst_ref=s_ref.at[piece, :],
+                send_sem=g_sem.at[0, k - 1],
+                recv_sem=g_sem.at[1, k - 1],
+                device_id=plane_peer(k)[1],
+                device_id_type=MESH,
+            )
+        )
+        copies[-1].start()
+    s_ref[piece, :] = total
+    for copy in copies:
+        copy.wait()
+
+
+def exchange_and_gram(y4, grids, bands, atoms, cells):
+    blocks, rows, nb, width = y4.shape
+    size = bands * nb
+    plane = bands * atoms
+    depth = size // plane
+    vmem = pl.BlockSpec(memory_space=pltpu.VMEM)
+    return pl.pallas_call(
+        functools.partial(gram_kernel, grids, bands, atoms, 1.0 / cells),
+        out_shape=(
+            jax.ShapeDtypeStruct((rows, size, width), jnp.float32),
+            jax.ShapeDtypeStruct((size, size), jnp.float32),
+        ),
+        in_specs=[vmem],
+        out_specs=(vmem, vmem),
+        scratch_shapes=[
+            pltpu.VMEM((plane, depth, size), jnp.float32),
+            pltpu.VMEM((plane - 1, depth, size), jnp.float32),
+            pltpu.VMEM((grids, depth, size), jnp.float32),
+            pltpu.VMEM((depth, size), jnp.float32),
+            pltpu.SemaphoreType.DMA((2, bands - 1)),
+            pltpu.SemaphoreType.DMA((2, plane - 1)),
+            pltpu.SemaphoreType.DMA((2, grids - 1)),
+            pltpu.SemaphoreType.DMA((2, plane - 1)),
+        ],
+        compiler_params=pltpu.CompilerParams(
+            collective_id=0, has_side_effects=True, vmem_limit_bytes=56 << 20
+        ),
+    )(y4)
+
+
+def factor_kernel(step, s_ref, x_ref, work):
+    size = s_ref.shape[0]
+    work[:, :size] = s_ref[...]
+    rows = lax.broadcasted_iota(jnp.int32, (size, size), 0)
+    cols = lax.broadcasted_iota(jnp.int32, (size, size), 1)
+    work[:, size:] = jnp.where(rows == cols, 1.0, 0.0)
+    row = lax.broadcasted_iota(jnp.int32, (step, 1), 0)
+    eye = jnp.where(
+        lax.broadcasted_iota(jnp.int32, (step, step), 0)
+        == lax.broadcasted_iota(jnp.int32, (step, step), 1),
+        1.0,
+        0.0,
+    )
+    for k in range(size // step):
+        lo, hi = k * step, (k + 1) * step
+        pair = jnp.concatenate([work[lo:hi, lo:hi], eye], axis=1)
+        scales = jnp.zeros((step, 1), jnp.float32)
+        for j in range(step):
+            line = pair[j : j + 1, :]
+            pivot = pair[j : j + 1, j : j + 1]
+            column = pair[:, j : j + 1]
+            scales = jnp.where(row == j, lax.rsqrt(pivot), scales)
+            ratio = jnp.where(row > j, column / pivot, 0.0)
+            pair = pair - ratio * line
+        inverse = pair[:, step:] * scales
+        block = mm6(inverse, work[lo:hi, :])
+        x_ref[lo:hi, :] = block[:, size:]
+        if hi < size:
+            work[hi:, :] = work[hi:, :] - mm6(block[:, hi:size], block, ((0,), (0,)))
+
+
+def mm6(a, b, dims=((1,), (0,))):
+    return lax.dot_general(
+        a, b, (dims, ((), ())), precision=HIGHEST, preferred_element_type=jnp.float32
+    )
+
+
+def inverse_factor(s, step):
+    size = s.shape[0]
+    vmem = pl.BlockSpec(memory_space=pltpu.VMEM)
+    return pl.pallas_call(
+        functools.partial(factor_kernel, step),
+        out_shape=jax.ShapeDtypeStruct((size, size), jnp.float32),
+        in_specs=[vmem],
+        out_specs=vmem,
+        scratch_shapes=[pltpu.VMEM((size, 2 * size), jnp.float32)],
+    )(s)
+
+
+def combine_kernel(bands, x_ref, yq_ref, o_ref, z, s_sem, r_sem):
+    g, b, c = lax.axis_index("grid"), lax.axis_index("band"), lax.axis_index("atom")
+    rows, size, width = yq_ref.shape
+    nb = size // bands
+    barrier = pltpu.get_barrier_semaphore()
+    for k in range(1, bands):
+        pl.semaphore_signal(
+            barrier, inc=1, device_id=device(g, lax.rem(b + k, bands), c), device_id_type=MESH
+        )
+    pl.semaphore_wait(barrier, bands - 1)
+    copies = []
+    for r in range(rows):
+        z[r] = mm3(x_ref[...], yq_ref[r])
+        for k in range(1, bands):
+            p = lax.rem(b + k, bands)
+            copies.append(
+                pltpu.make_async_remote_copy(
+                    src_ref=z.at[r, pl.ds(pl.multiple_of(p * nb, nb), nb), :],
+                    dst_ref=o_ref.at[b, r],
+                    send_sem=s_sem.at[r, k - 1],
+                    recv_sem=r_sem.at[r, k - 1],
+                    device_id=device(g, p, c),
+                    device_id_type=MESH,
+                )
+            )
+            copies[-1].start()
+    o_ref[b] = z[:, pl.ds(pl.multiple_of(b * nb, nb), nb), :]
+    for copy in copies:
+        copy.wait()
+
+
+def combine_and_return(x, yq, bands):
+    rows, size, width = yq.shape
+    vmem = pl.BlockSpec(memory_space=pltpu.VMEM)
+    return pl.pallas_call(
+        functools.partial(combine_kernel, bands),
+        out_shape=jax.ShapeDtypeStruct((bands, rows, size // bands, width), jnp.float32),
+        in_specs=[vmem, vmem],
+        out_specs=vmem,
+        scratch_shapes=[
+            pltpu.VMEM((rows, size, width), jnp.float32),
+            pltpu.SemaphoreType.DMA((rows, bands - 1)),
+            pltpu.SemaphoreType.DMA((rows, bands - 1)),
+        ],
+        compiler_params=pltpu.CompilerParams(
+            collective_id=1, has_side_effects=True, vmem_limit_bytes=56 << 20
+        ),
+    )(x, yq)
 
 
 def from_behind(block, axis, distance):
@@ -40,12 +303,6 @@
         after = lax.ppermute(first, axis, down)
         x = jnp.concatenate([before, x, after], axis=dim)
     return x
-
-
-def inner_rows(left, right):
-    return lax.dot_general(
-        left, right, (((1,), (1,)), ((), ())), precision=HIGHEST, preferred_element_type=jnp.float32
-    )
 
 
 def spread_terms(weighted, projectors, sphere_index, total_cells):
@@ -105,25 +362,14 @@
         fold_rims(dense, depth), "atom", scatter_dimension=1, tiled=True
     )
     updated = centre - STEP_SIZE * (KINETIC * laplace + potential * centre + nonlocal_half)
-    flat_rows = updated.reshape(band_rows, half * plane_cells)
-    cells_total = lax.axis_size("grid") * depth * plane_cells
-    block = inner_rows(flat_rows, lax.all_gather(flat_rows, "band", axis=0, tiled=True))
-    summed_rows = lax.psum(block, ("grid", "atom")) / cells_total
-    intersection_matrix = lax.all_gather(summed_rows, "band", axis=0, tiled=True)
-    factor = jnp.linalg.cholesky(intersection_matrix)
-    inverse = lax.linalg.triangular_solve(
-        factor, jnp.eye(BANDS, dtype=jnp.float32), left_side=True, lower=True
-    )
-    own_inverse = lax.dynamic_slice_in_dim(
-        inverse, lax.axis_index("band") * band_rows, band_rows, 0
-    )
-    result = jnp.dot(
-        own_inverse,
-        lax.all_gather(flat_rows, "band", axis=0, tiled=True),
-        precision=HIGHEST,
-        preferred_element_type=jnp.float32,
-    )
-    return result.reshape(band_rows, half, plane_cells)
+    grids, bands = lax.axis_size("grid"), lax.axis_size("band")
+    cells_total = grids * depth * plane_cells
+    width = plane_cells // bands
+    y4 = updated.reshape(band_rows, half, bands, width).transpose(2, 1, 0, 3)
+    gathered, intersection_matrix = exchange_and_gram(y4, grids, bands, groups, cells_total)
+    inverse = inverse_factor(intersection_matrix, band_rows)
+    pieces = combine_and_return(inverse, gathered, bands)
+    return pieces.transpose(2, 1, 0, 3).reshape(band_rows, half, plane_cells)
 
 
 def solution(mesh):

time: 551 us -> 421 us (0.76)
  waiting for transfers between devices: 247 us -> 104 us
  Pallas kernels: 0 us -> 105 us
  other arithmetic: 128 us -> 72.5 us
  matrix products: 23.2 us -> 3.68 us
  blocking collectives: 9.45 us -> 0 us
    pallas_call x0 -> x3, Pallas kernels: none -> 105 us  [the longest x1 47.2 us: exchange_and_gram(): pl.pallas_call(functools.partial(gram_kernel, grids, bands, atoms, 1.0 /...]
    all_gather x1 -> x0, waiting for transfers between devices: 88.8 us -> none  [body(): lax.all_gather(flat_rows, 'band', axis=0, tiled=True)]
    psum x1 -> x0, waiting for transfers between devices: 54.8 us -> none  [body(): summed_rows = lax.psum(block, ('grid', 'atom')) / cells_total]
    another operation x10 -> x0, other arithmetic: 54.3 us -> none  [the longest x7 34.6 us: body(): factor = jnp.linalg.cholesky(intersection_matrix)]
    dot_general x2 -> x0, matrix products: 18.2 us -> none  [the longest x1 10.7 us: inner_rows(): lax.dot_general(left, right, (((1,), (1,)), ((), ())), precision=HIGHEST,...]
    sub x0 -> x1, other arithmetic: none -> 15.7 us  [body(): centre - STEP_SIZE * (KINETIC * laplace + potential * centre + nonlocal_h...]
    unnamed x3 -> x1, other arithmetic: 15.7 us -> 0.01 us
    all_gather x1 -> x0, blocking collectives: 9.45 us -> none  [body(): lax.all_gather(summed_rows, 'band', axis=0, tiled=True)]
  transfers between devices with their start and end apart: 7 -> 5, of which waited for: 7 -> 5; matrix products, arithmetic and copies ran while one was open for 6% -> 8% of each run, Pallas kernels for 0% -> 0%
where the time goes in v1:
time: 421 us; the launch traced here: 420 us
  local copies, waits for them, and re-layouts  105 us (25%)
  Pallas kernels  105 us (25%)
  waiting for transfers between devices  104 us (25%)
  other arithmetic  72.5 us (17%)
  starting transfers between devices  16.5 us (4%)
  between operations  14.3 us (3%)
    scatter-add x1, other arithmetic, spread_terms(): dense.at[:, sphere_index.reshape(-1)].add(values.reshape(band_rows, -1))  50.4 us
    pallas_call x1, Pallas kernels, exchange_and_gram(): pl.pallas_call(functools.partial(gram_kernel, grids, bands, atoms, 1.0 /...  47.2 us
    ppermute x2, waiting for transfers between devices, from_behind(): return lax.ppermute(block, axis, route)  38.6 us
    gather x2, local copies, waits for them, and re-layouts, body(): points = flattened[:, own_index]  35.7 us
    ppermute x1, waiting for transfers between devices, extended_2(): before = lax.ppermute(last, axis, up)  33.3 us
    pallas_call x1, Pallas kernels, combine_and_return(): pl.pallas_call(functools.partial(combine_kernel, bands), out_shape=jax.Sh...  30.2 us
    pallas_call x1, Pallas kernels, inverse_factor(): pl.pallas_call(functools.partial(factor_kernel, step), out_shape=jax.Shap...  27.2 us
    unnamed x22, local copies, waits for them, and re-layouts  26.7 us
  transfers between devices with their start and end apart: 5, of which 5 were waited for; matrix products, arithmetic and copies ran while one was open for 8% of the time, Pallas kernels for 0%

profile of v1, /device:TPU:0, one launch (start us, length us, event | category | flops | bytes accessed | tf_op | source)
XLA Modules:
  0.0 420.4 jit_solution(16875625150969208035)
XLA Ops:
  6.5 0.0 copy-start
  6.5 0.0 reduce-scatter.2.cloned.1.call-start
  6.5 2.7 fusion.80
  9.3 0.9 copy.50
  10.2 0.0 copy-start.4
  10.2 0.0 copy-start.5
  10.2 3.1 collective-permute-start
  13.3 0.9 copy.51
  14.2 2.3 collective-permute-start.1
  17.3 0.1 fusion.78
  17.4 0.1 copy.28
  17.5 33.3 %collective-permute-done = f32[64,6,1024]{2,0,1:T(8,128)} collective-permute-done((f32[64,6,1024]{2,0,1:T(8,128)S(1)}, f32[64,6,1024]{2,0,1:T(8,128)}, u32[]{:S(2)}, u32[]{:S(2)}) %collective-permute-start) | collective-permute-done | bytes 1572896 | tf_op jit(solution)/shard_map/ppermute | solution.py:302
  50.7 2.7 constant_dynamic-update-slice_fusion.2
  53.5 6.6 %constant_dynamic-update-slice_fusion.1 = f32[64,28,1024]{2,0,1:T(8,128)} fusion(f32[64,28,1024]{2,0,1:T(8,128)} %constant_dynamic-update-slice_fusion.2, f32[64,16,1024]{2,1,0:T(8,128)} %param.10), kind=kLoop, calls=%fused_computation.104 | loop fusion | bytes 8388608
  60.1 23.5 %collective-permute-done.1 = f32[64,6,1024]{2,0,1:T(8,128)} collective-permute-done((f32[64,6,1024]{2,0,1:T(8,128)S(1)}, f32[64,6,1024]{2,0,1:T(8,128)}, u32[]{:S(2)}, u32[]{:S(2)}) %collective-permute-start.1) | collective-permute-done | bytes 1572896 | tf_op jit(solution)/shard_map/ppermute | solution.py:303
  83.5 2.8 constant_dynamic-update-slice_fusion
  86.4 11.1 %copy.26 = f32[64,28,1024]{0,2,1:T(8,128)} copy(f32[64,28,1024]{2,0,1:T(8,128)} %constant_dynamic-update-slice_fusion) | data formatting | bytes 14680064 | tf_op jit(solution)/shard_map/concatenate | solution.py:304
  97.5 32.9 %gather_fusion = f32[8192,64]{1,0:T(8,128)} fusion(f32[64,28672]{0,1:T(8,128)} %bitcast.40, s32[8192]{0:T(1024)S(1)} %broadcast_clamp_fusion), kind=kCustom, calls=%fused_computation | custom fusion | bytes 4227072 | tf_op jit(solution)/shard_map/gather | solution.py:353
  130.3 2.8 copy.27
  133.2 1.8 fusion.61
  135.0 1.9 convolution_bitcast_fusion
  136.9 0.2 copy.45
  137.1 2.7 copy.30
  139.8 50.4 %scatter_custom_fusion = f32[64,28672]{0,1:T(8,128)} fusion(s32[8192]{0:T(1024)S(1)} %bitcast.48, f32[8192,64]{1,0:T(8,128)} %copy.30, f32[]{:T(128)} %constant.103.clone.1), kind=kCustom, calls=%fused_computation.26 | custom fusion | flops 524288 | bytes 7340544 | tf_op jit(solution)/shard_map/scatter-add | solution.py:312
  190.2 7.1 %fusion.79 = (f32[64,6,1024]{0,2,1:T(8,128)}, f32[64,6,1024]{0,2,1:T(8,128)}, f32[64,6,1024]{0,2,1:T(8,128)S(1)}) fusion(f32[64,28,1024]{0,2,1:T(8,128)} %bitcast.38), kind=kLoop, calls=%fused_computation.130 | loop fusion | bytes 9437184 | tf_op jit(solution)/shard_map/slice | solution.py:317
  197.3 3.2 copy.42
  200.6 0.6 collective-permute-start.2
  201.1 3.2 copy.43
  204.4 10.5 %collective-permute-start.3 = (f32[64,6,1024]{2,0,1:T(8,128)}, f32[64,6,1024]{2,0,1:T(8,128)}, u32[]{:S(2)}, u32[]{:S(2)}) collective-permute-start(f32[64,6,1024]{2,0,1:T(8,128)} %copy.43), channel_id=1, source_target_pairs={{8,0},{16,8},{24,16},{0,24},{9,1},{17,9},{25,17},{1,25},{10,2},{18... | collective-permute-start | bytes 4718600 | tf_op jit(solution)/shard_map/ppermute | solution.py:292
  214.9 7.5 %slice.223 = f32[64,16,1024]{0,2,1:T(8,128)} slice(f32[64,28,1024]{0,2,1:T(8,128)} %bitcast.39), slice={[0:64], [6:22], [0:1024]} | slice | bytes 8388608 | tf_op jit(solution)/shard_map/slice | solution.py:318
  222.3 2.0 copy.41
  224.4 6.9 %copy.40 = f32[64,16,1024]{2,0,1:T(8,128)} copy(f32[64,16,1024]{0,2,1:T(8,128)} %slice.223) | data formatting | bytes 8388608
  231.3 15.9 %collective-permute-done.2 = f32[64,6,1024]{2,0,1:T(8,128)} collective-permute-done((f32[64,6,1024]{2,0,1:T(8,128)}, f32[64,6,1024]{2,0,1:T(8,128)}, u32[]{:S(2)}, u32[]{:S(2)}) %collective-permute-start.2) | collective-permute-done | bytes 1572896 | tf_op jit(solution)/shard_map/ppermute | solution.py:292
  247.2 2.8 add_dynamic-update-slice_fusion
  250.0 22.7 %collective-permute-done.3 = f32[64,6,1024]{2,0,1:T(8,128)} collective-permute-done((f32[64,6,1024]{2,0,1:T(8,128)}, f32[64,6,1024]{2,0,1:T(8,128)}, u32[]{:S(2)}, u32[]{:S(2)}) %collective-permute-start.3) | collective-permute-done | bytes 1572896 | tf_op jit(solution)/shard_map/ppermute | solution.py:292
  272.7 3.4 fusion.57
  276.1 0.0 reduce-scatter.2.cloned.1.call-update
  276.2 0.0 copy-start.3
  276.3 1.7 constant_dynamic-slice_fusion
  278.0 8.6 %reduce-scatter.2.cloned.1.call-done = f32[64,8,1024]{2,0,1:T(8,128)} async-done(((f32[64,16,1024]{2,0,1:T(8,128)}), f32[64,8,1024]{2,0,1:T(8,128)}) %reduce-scatter.2.cloned.1.call-update) | async-done | bytes 2097168 | tf_op jit(solution)/shard_map/reduce_scatter | solution.py:361
  286.6 15.7 %fusion.17 = f32[64,8,1024]{2,0,1:T(8,128)S(1)} fusion(f32[64,8,1024]{2,0,1:T(8,128)S(1)} %constant_dynamic-slice_fusion, f32[64,8,1024]{2,0,1:T(8,128)} %reduce-scatter.2.cloned.1.call-done, f32[64,28,1024]{2,0,1:T(8,128)} %constant_dynamic-update-slice_fusion, s32[]{:T(128)S(6)} %select_n.87, s32[]{:T(128)S(6)} %add.271, s32[]{:T(128)S(6)} %add.270, ...), kind=kLoop, calls=%fused_computation.43 | loop fusion | flops 31981568 | bytes 31502384 | tf_op jit(solution)/shard_map/sub | solution.py:364
  302.3 1.6 copy.52
  303.9 47.2 %shard_map.64 = (f32[8,256,256]{2,1,0:T(8,128)}, f32[256,256]{1,0:T(8,128)}) custom-call(f32[4,8,64,256]{3,2,1,0:T(8,128)} %bitcast.44), custom_call_target="tpu_custom_call" | custom-call | tf_op jit(solution)/shard_map/pallas_call | solution.py:166
  351.1 27.2 %shard_map.65.x_ref = f32[256,256]{1,0:T(8,128)} custom-call(f32[256,256]{1,0:T(8,128)} %get-tuple-element.31.s_ref), custom_call_target="tpu_custom_call" | custom-call | tf_op jit(solution)/shard_map/pallas_call | solution.py:230
  378.3 30.2 %shard_map.66 = f32[4,8,64,256]{3,2,1,0:T(8,128)} custom-call(f32[256,256]{1,0:T(8,128)} %shard_map.65.x_ref, f32[8,256,256]{2,1,0:T(8,128)} %get-tuple-element.32.yq_ref), custom_call_target="tpu_custom_call" | custom-call | tf_op jit(solution)/shard_map/pallas_call | solution.py:273
  408.4 0.0 copy-start.1
  408.4 3.0 copy.37
  411.4 2.1 reshape.118
  (20 shorter events, 0.2 us)
Async XLA Ops:
  6.5 126.6 %copy-start = (f32[32,4,512]{2,1,0:T(4,128)S(1)}, f32[32,4,512]{2,1,0:T(4,128)}, u32[]{:S(2)}) copy-start(f32[32,4,512]{2,1,0:T(4,128)} %param.12) | copy-start | bytes 786436
  6.5 280.0 %reduce-scatter.2.cloned.1.call-start = ((), (), s32[]{:S(2)}) async-start(), calls=%async_computation.1 | async-start | bytes 6291456 | tf_op jit(solution)/shard_map/reduce_scatter | solution.py:361
  10.2 6.3 %copy-start.4 = (s32[32,512]{1,0:T(8,128)S(1)}, s32[32,512]{1,0:T(8,128)}, u32[]{:S(2)}) copy-start(s32[32,512]{1,0:T(8,128)} %param.14) | copy-start | bytes 196612
  10.2 7.1 %copy-start.5 = (f32[32,4]{0,1:T(4,128)S(1)}, f32[32,4]{0,1:T(4,128)}, u32[]{:S(2)}) copy-start(f32[32,4]{0,1:T(4,128)} %param.13) | copy-start | bytes 1540
  10.2 40.5 %collective-permute-start = (f32[64,6,1024]{2,0,1:T(8,128)S(1)}, f32[64,6,1024]{2,0,1:T(8,128)}, u32[]{:S(2)}, u32[]{:S(2)}) collective-permute-start(f32[64,6,1024]{2,0,1:T(8,128)S(1)} %copy.50), channel_id=1, source_target_pairs={{0,8},{8,16},{16,24},{24,0},{1,9},{9,17},{17,25},{25,1},{2,10},{10... | collective-permute-start | bytes 4718600 | tf_op jit(solution)/shard_map/ppermute | solution.py:302
  14.2 69.3 %collective-permute-start.1 = (f32[64,6,1024]{2,0,1:T(8,128)S(1)}, f32[64,6,1024]{2,0,1:T(8,128)}, u32[]{:S(2)}, u32[]{:S(2)}) collective-permute-start(f32[64,6,1024]{2,0,1:T(8,128)S(1)} %copy.51), channel_id=1, source_target_pairs={{8,0},{16,8},{24,16},{0,24},{9,1},{17,9},{25,17},{1,25},{10,2},{18... | collective-permute-start | bytes 4718600 | tf_op jit(solution)/shard_map/ppermute | solution.py:303
  200.6 46.6 %collective-permute-start.2 = (f32[64,6,1024]{2,0,1:T(8,128)}, f32[64,6,1024]{2,0,1:T(8,128)}, u32[]{:S(2)}, u32[]{:S(2)}) collective-permute-start(f32[64,6,1024]{2,0,1:T(8,128)} %copy.42), channel_id=1, source_target_pairs={{24,0},{0,8},{8,16},{16,24},{25,1},{1,9},{9,17},{17,25},{26,2},{2,... | collective-permute-start | bytes 4718600 | tf_op jit(solution)/shard_map/ppermute | solution.py:292
  204.4 68.4 %collective-permute-start.3 = (f32[64,6,1024]{2,0,1:T(8,128)}, f32[64,6,1024]{2,0,1:T(8,128)}, u32[]{:S(2)}, u32[]{:S(2)}) collective-permute-start(f32[64,6,1024]{2,0,1:T(8,128)} %copy.43), channel_id=1, source_target_pairs={{8,0},{16,8},{24,16},{0,24},{9,1},{17,9},{25,17},{1,25},{10,2},{18... | collective-permute-start | bytes 4718600 | tf_op jit(solution)/shard_map/ppermute | solution.py:292
  224.4 22.8 %copy-start.2 = (f32[64,6,1024]{2,0,1:T(8,128)S(1)}, f32[64,6,1024]{2,0,1:T(8,128)}, u32[]{:S(2)}) copy-start(f32[64,6,1024]{2,0,1:T(8,128)} %copy.41) | copy-start | bytes 4718596
  276.2 10.3 %copy-start.3 = (f32[8,1024]{1,0:T(8,128)S(1)}, f32[8,1024]{1,0:T(8,128)}, u32[]{:S(2)}) copy-start(f32[8,1024]{1,0:T(8,128)} %param.11) | copy-start | bytes 98308
  408.4 5.1 %copy-start.1 = (f32[32,4,512]{2,1,0:T(4,128)S(1)}, f32[32,4,512]{2,1,0:T(4,128)}, u32[]{:S(2)}) copy-start(f32[32,4,512]{2,1,0:T(4,128)} %param.12) | copy-start | bytes 786436
Sparse Core Ops, SparseCore 0:
  276.3 10.2 reduce-scatter.1

commit v2 on v1

--- a/solution.py
+++ b/solution.py
@@ -286,86 +286,252 @@
     )(x, yq)
 
 
-def from_behind(block, axis, distance):
-    devices = range(lax.axis_size(axis))
-    route = [((i - distance) % len(devices), i) for i in devices]
-    return lax.ppermute(block, axis, route)
-
-
-def extended_2(x, sides, width):
-    for axis, dim in sides:
-        count, length = (lax.axis_size(axis), x.shape[dim])
-        up = [(i, (i + 1) % count) for i in range(count)]
-        down = [(j, i) for i, j in up]
-        last = lax.slice_in_dim(x, length - width, length, axis=dim)
-        first = lax.slice_in_dim(x, 0, width, axis=dim)
-        before = lax.ppermute(last, axis, up)
-        after = lax.ppermute(first, axis, down)
-        x = jnp.concatenate([before, x, after], axis=dim)
-    return x
-
-
-def spread_terms(weighted, projectors, sphere_index, total_cells):
-    band_rows = weighted.shape[0]
-    values = jnp.einsum("nai,ais->nas", weighted, projectors, precision=HIGHEST)
-    dense = jnp.zeros((band_rows, total_cells), jnp.float32)
-    return dense.at[:, sphere_index.reshape(-1)].add(values.reshape(band_rows, -1))
-
-
-def fold_rims(dense, depth):
-    from_below = from_behind(dense[:, depth + 6 :], "grid", 1)
-    from_above = from_behind(dense[:, :6], "grid", -1)
-    inner = dense[:, 6 : depth + 6]
-    inner = inner.at[:, :6].add(from_below)
-    return inner.at[:, depth - 6 :].add(from_above)
+def plane_kernel(core_rows, rows_ref, potential_ref, base_ref, weights):
+    depth, nb, cells = rows_ref.shape
+    half = base_ref.shape[0]
+    tile = weights.shape[1]
+    reach = tile // CY
+    shape = weights.shape
+    source = lax.broadcasted_iota(jnp.int32, shape, 0) - tile
+    target = lax.broadcasted_iota(jnp.int32, shape, 1)
+    dx = jnp.abs((source + tile) // CY - reach - target // CY)
+    dy = jnp.abs((source + tile) % CY - target % CY)
+    value = jnp.zeros(shape, jnp.float32)
+    for k in range(1, 7):
+        hit = ((dx == k) & (dy == 0)) | ((dx == 0) & (dy == k))
+        value = jnp.where(hit, STENCIL[k], value)
+    weights[...] = value
+    first = lax.axis_index("atom") * core_rows
+
+    def one(k, carry):
+        for t in range(cells // tile):
+            here = slice(t * tile, (t + 1) * tile)
+            low, high = max(t - 1, 0), min(t + 2, cells // tile)
+            field = rows_ref[first + k, :, low * tile : high * tile]
+            band = weights[(low - t + 1) * tile : (high - t + 1) * tile, :]
+            plane = mm3(field, band)
+            centre = rows_ref[first + k, :, here]
+            applied = KINETIC * (3.0 * STENCIL[0] * centre + plane)
+            applied = applied + potential_ref[pl.ds(k, 1), here] * centre
+            base_ref[k, :, here] = centre - STEP_SIZE * applied
+        return carry
+
+    lax.fori_loop(0, half, one, 0)
+
+
+def plane_part(rows, potential):
+    depth, nb, cells = rows.shape
+    half = potential.shape[0]
+    vmem = pl.BlockSpec(memory_space=pltpu.VMEM)
+    tile = 8 * CY
+    return pl.pallas_call(
+        functools.partial(plane_kernel, half),
+        out_shape=jax.ShapeDtypeStruct((half, nb, cells), jnp.float32),
+        in_specs=[vmem, vmem],
+        out_specs=vmem,
+        scratch_shapes=[pltpu.VMEM((3 * tile, tile), jnp.float32)],
+        compiler_params=pltpu.CompilerParams(vmem_limit_bytes=56 << 20),
+        cost_estimate=pl.CostEstimate(
+            flops=12 * half * nb * cells * tile, bytes_accessed=40 * nb * half * cells, transcendentals=0
+        ),
+    )(rows, potential)
+
+
+def dense_kernel(
+    extra, table_ref, cubes_ref, rows_ref, sums_ref, near_hi, near_lo, rim_hi, rim_lo, dense
+):
+    core = lax.axis_index("atom")
+    half, projectors, cells = near_hi.shape
+    depth = rows_ref.shape[0]
+    window = depth + extra
+    atoms = table_ref.shape[1]
+    each = projectors // atoms
+    planes = cubes_ref.shape[1] // each
+
+    def clear(w, carry):
+        dense[w] = jnp.zeros((projectors, cells), jnp.float32)
+        return carry
+
+    lax.fori_loop(0, window, clear, 0)
+    pair = 8 // each
+
+    def build(p, carry):
+        for h in range(pair):
+            atom = p * pair + h
+
+            @pl.when(table_ref[2, atom] > 0)
+            def _():
+                cube = cubes_ref[atom]
+                rest = jnp.zeros((cube.shape[0], cells - cube.shape[1]), jnp.float32)
+                moved = pltpu.roll(jnp.concatenate([cube, rest], axis=1), table_ref[1, atom], 1)
+                start = table_ref[0, atom]
+                group = dense.at[:, pl.ds(pl.multiple_of(p * 8, 8), 8), :]
+                for e in range(planes):
+                    group[start + e, h * each : (h + 1) * each, :] = moved[
+                        e * each : (e + 1) * each, :
+                    ]
+
+        return carry
+
+    lax.fori_loop(0, atoms // pair, build, 0)
+    ahead = extra * (1 - core)
+    sums_ref[...] = jnp.zeros_like(sums_ref)
+
+    def gather(r, carry):
+        sums_ref[...] += mm3(rows_ref[r], dense[r + ahead], ((1,), (1,)))
+        return carry
+
+    lax.fori_loop(0, depth, gather, 0)
+    own = extra + (half - extra) * core
+
+    def keep_near(k, carry):
+        near_hi[k], near_lo[k] = split(dense[own + k])
+        return carry
+
+    def keep_rim(k, carry):
+        rim_hi[k], rim_lo[k] = split(dense[depth * core + k])
+        return carry
+
+    lax.fori_loop(0, half, keep_near, 0)
+    lax.fori_loop(0, extra, keep_rim, 0)
+
+
+def dense_projectors(table, cubes, rows, half, extra, each):
+    depth, nb, cells = rows.shape
+    projectors = table.shape[1] * each
+    vmem = pl.BlockSpec(memory_space=pltpu.VMEM)
+    near = jax.ShapeDtypeStruct((half, projectors, cells), jnp.bfloat16)
+    rim = jax.ShapeDtypeStruct((extra, projectors, cells), jnp.bfloat16)
+    return pl.pallas_call(
+        functools.partial(dense_kernel, extra),
+        out_shape=(jax.ShapeDtypeStruct((nb, projectors), jnp.float32), near, near, rim, rim),
+        in_specs=[pl.BlockSpec(memory_space=pltpu.SMEM), vmem, vmem],
+        out_specs=(vmem,) * 5,
+        scratch_shapes=[pltpu.VMEM((depth + extra, projectors, cells), jnp.float32)],
+        compiler_params=pltpu.CompilerParams(vmem_limit_bytes=60 << 20),
+        cost_estimate=pl.CostEstimate(
+            flops=6 * depth * nb * cells * projectors,
+            bytes_accessed=4 * (depth + half) * projectors * cells,
+            transcendentals=0,
+        ),
+    )(table, cubes, rows)
+
+
+def update_kernel(
+    halo_ref, base_ref, rows_ref, sums_ref, scale_ref, near_hi, near_lo, rim_hi, rim_lo, y_ref, window
+):
+    core = lax.axis_index("atom")
+    extra, nb, cells = halo_ref.shape
+    depth = rows_ref.shape[0]
+    half = base_ref.shape[0]
+    blocks, width = y_ref.shape[0], y_ref.shape[3]
+    ahead = extra * (1 - core)
+
+    def put_rows(r, carry):
+        window[r + ahead] = rows_ref[r]
+        return carry
+
+    def put_halo(k, carry):
+        window[depth * core + k] = halo_ref[k]
+        return carry
+
+    lax.fori_loop(0, depth, put_rows, 0)
+    lax.fori_loop(0, extra, put_halo, 0)
+
+    def gather(k, total):
+        hi, lo = split(halo_ref[k])
+        dims = ((1,), (1,))
+        return total + mm(hi, rim_hi[k], dims) + mm(lo, rim_hi[k], dims) + mm(hi, rim_lo[k], dims)
+
+    total = lax.fori_loop(0, extra, gather, sums_ref[...])
+    hi, lo = split(total * scale_ref[...])
+    own = extra + (half - extra) * core
+
+    def one(k, carry):
+        nonlocal_row = mm(hi, near_hi[k]) + mm(lo, near_hi[k]) + mm(hi, near_lo[k])
+        row = base_ref[k] - STEP_SIZE * nonlocal_row
+        for d in range(1, 7):
+            pair = window[own + k + d] + window[own + k - d]
+            row = row - (STEP_SIZE * KINETIC * STENCIL[d]) * pair
+        for b in range(blocks):
+            y_ref[b, k] = row[:, b * width : (b + 1) * width]
+        return carry
+
+    lax.fori_loop(0, half, one, 0)
+
+
+def update(halo, base, rows, sums, scale, near_hi, near_lo, rim_hi, rim_lo, blocks):
+    extra, nb, cells = halo.shape
+    half, depth = base.shape[0], rows.shape[0]
+    vmem = pl.BlockSpec(memory_space=pltpu.VMEM)
+    return pl.pallas_call(
+        update_kernel,
+        out_shape=jax.ShapeDtypeStruct((blocks, half, nb, cells // blocks), jnp.float32),
+        in_specs=[vmem] * 9,
+        out_specs=vmem,
+        scratch_shapes=[pltpu.VMEM((depth + extra, nb, cells), jnp.float32)],
+        compiler_params=pltpu.CompilerParams(vmem_limit_bytes=56 << 20),
+    )(halo, base, rows, sums, scale, near_hi, near_lo, rim_hi, rim_lo)
+
+
+def in_cube_order(projectors, sphere_index, edge, plane_cells):
+    cell = lax.iota(jnp.int32, edge * edge * edge)
+    offset = cell // (edge * edge) * plane_cells + cell // edge % edge * CY + cell % edge
+    first = jnp.min(sphere_index, axis=1, keepdims=True)
+    ordered = jnp.all(sphere_index == first + offset[None])
+
+    def arrange(values):
+        order = jnp.argsort(sphere_index, axis=1)
+        return jnp.take_along_axis(values, order[:, None, :], axis=2)
+
+    return lax.cond(ordered, lambda values: values, arrange, projectors), first[:, 0]
 
 
 def body(psi, potential, projectors, strength, sphere_index, atom_count):
     band_rows, depth, plane_cells = psi.shape
-    groups = lax.axis_size("atom")
+    groups, grids, bands = (lax.axis_size(name) for name in ("atom", "grid", "band"))
     core = lax.axis_index("atom")
     half = depth // groups
-    extended = extended_2(psi, (("grid", 1),), 6)
-    window = lax.dynamic_slice_in_dim(extended, core * half, half + 12, 1)
-    centre = window[:, 6 : 6 + half]
-    margin = 6 * CY
-    padded = jnp.pad(centre, ((0, 0), (0, 0), (margin, margin)))
-    column = lax.iota(jnp.int32, plane_cells) % CY
-    laplace = 3.0 * STENCIL[0] * centre
-    for k in range(1, 7):
-        along_z = window[:, 6 + k : 6 + k + half] + window[:, 6 - k : 6 - k + half]
-        along_x = (
-            padded[:, :, margin + k * CY : margin + k * CY + plane_cells]
-            + padded[:, :, margin - k * CY : margin - k * CY + plane_cells]
-        )
-        upper = jnp.where(column + k < CY, padded[:, :, margin + k : margin + k + plane_cells], 0.0)
-        lower = jnp.where(column >= k, padded[:, :, margin - k : margin - k + plane_cells], 0.0)
-        laplace = laplace + STENCIL[k] * (along_z + along_x + upper + lower)
-    atom_slots = sphere_index.shape[0]
-    share = atom_slots // groups
+    atom_slots, each, points = projectors.shape
+    edge = round(points ** (1 / 3))
+    extra = edge - 1
+    route = []
+    for i in range(grids):
+        route.append((i * groups + 1, (i + 1) % grids * groups))
+        route.append((i * groups, (i - 1) % grids * groups + 1))
+
+    ordered, first = in_cube_order(projectors, sphere_index, edge, plane_cells)
     alive_mask = (lax.iota(jnp.int32, atom_slots) < atom_count[0]).astype(jnp.float32)
-    scaled = strength * alive_mask[:, None]
-    flattened = extended.reshape(band_rows, -1)
-    total_cells = flattened.shape[1]
-    own_index = lax.dynamic_slice_in_dim(sphere_index, core * share, share, 0)
-    own_projectors = lax.dynamic_slice_in_dim(projectors, core * share, share, 0)
-    own_scaled = lax.dynamic_slice_in_dim(scaled, core * share, share, 0)
-    points = flattened[:, own_index]
-    intersections = jnp.einsum(
-        "nas,ais->nai", points, own_projectors, precision=HIGHEST
-    ) / math.sqrt(projectors.shape[2])
-    weighted = intersections * own_scaled[None]
-    dense = spread_terms(weighted, own_projectors, own_index, total_cells).reshape(
-        band_rows, depth + 12, plane_cells
+    scaled = strength * alive_mask[:, None] / math.sqrt(points)
+    count = atom_slots * each
+    lines = -(-count // points)
+    scaled_line = jnp.pad(scaled.reshape(-1), (0, lines * points - count)).reshape(lines, points)
+    first_line = jnp.pad(first.astype(jnp.float32), (0, points - atom_slots))[None]
+    sent = jnp.concatenate([ordered.reshape(count, points), scaled_line, first_line], axis=0)
+    got = lax.ppermute(sent, ("grid", "atom"), route)
+    edge_rows = lax.dynamic_slice_in_dim(psi, core * (depth - extra), extra, 1).transpose(1, 0, 2)
+    halo = lax.ppermute(edge_rows, ("grid", "atom"), route)
+
+    rows = psi.transpose(1, 0, 2)
+    base = plane_part(rows, potential)
+    other_first = got[-1, :atom_slots].astype(jnp.int32)
+    other_scaled = got[count : count + lines].reshape(-1)[:count]
+    bottom = jnp.concatenate(
+        [first // plane_cells - 6, other_first // plane_cells - 6 + depth * (2 * core - 1)]
     )
-    nonlocal_half = lax.psum_scatter(
-        fold_rims(dense, depth), "atom", scatter_dimension=1, tiled=True
-    )
-    updated = centre - STEP_SIZE * (KINETIC * laplace + potential * centre + nonlocal_half)
-    grids, bands = lax.axis_size("grid"), lax.axis_size("band")
+    lane = jnp.concatenate([first % plane_cells, other_first % plane_cells])
+    touches = (bottom < half * (core + 1)) & (bottom + edge > half * core)
+    start = jnp.clip(bottom + extra * (1 - core), 0, depth + extra - edge)
+    table = jnp.stack([start, lane, touches.astype(jnp.int32)])
+    cubes = jnp.stack([ordered.reshape(count, points), got[:count]])
+    cubes = cubes.reshape(2 * atom_slots, each, edge, edge, edge).transpose(0, 2, 1, 3, 4)
+    cubes = jnp.pad(cubes, ((0, 0), (0, 0), (0, 0), (0, 0), (0, CY - edge)))
+    cubes = cubes.reshape(2 * atom_slots, edge * each, edge * CY)
+    dense = dense_projectors(table, cubes, rows, half, extra, each)
+    scale = jnp.concatenate([scaled.reshape(-1), other_scaled])[None]
+    y4 = update(halo, base, rows, dense[0], scale, *dense[1:], bands)
+
     cells_total = grids * depth * plane_cells
-    width = plane_cells // bands
-    y4 = updated.reshape(band_rows, half, bands, width).transpose(2, 1, 0, 3)
     gathered, intersection_matrix = exchange_and_gram(y4, grids, bands, groups, cells_total)
     inverse = inverse_factor(intersection_matrix, band_rows)
     pieces = combine_and_return(inverse, gathered, bands)

time: 421 us -> 222 us (0.53)
  waiting for transfers between devices: 104 us -> 0.01 us
  other arithmetic: 72.5 us -> 4.73 us
  local copies, waits for them, and re-layouts: 105 us -> 37.4 us
  Pallas kernels: 105 us -> 159 us
  starting transfers between devices: 16.5 us -> 4.6 us
    ppermute x4 -> x2, waiting for transfers between devices: 95.3 us -> 0.01 us  [the longest x1 0.01 us: body(): got = lax.ppermute(sent, ('grid', 'atom'), route)]
    scatter-add x3 -> x0, other arithmetic: 56.7 us -> none  [the longest x1 50.4 us: spread_terms(): dense.at[:, sphere_index.reshape(-1)].add(values.reshape(band_rows, -1))]
    pallas_call x0 -> x3, Pallas kernels: none -> 54.9 us  [the longest x1 24.9 us: dense_projectors(): pl.pallas_call(functools.partial(dense_kernel, extra), out_shape=(jax.Sha...]
    gather x2 -> x0, local copies, waits for them, and re-layouts: 35.7 us -> none  [body(): points = flattened[:, own_index]]
    slice x4 -> x1, local copies, waits for them, and re-layouts: 19 us -> 0.01 us  [body(): other_scaled = got[count:count + lines].reshape(-1)[:count]]
    sub x1 -> x0, other arithmetic: 15.7 us -> none  [body(): centre - STEP_SIZE * (KINETIC * laplace + potential * centre + nonlocal_h...]
    concatenate x2 -> x0, local copies, waits for them, and re-layouts: 13.9 us -> none  [extended_2(): x = jnp.concatenate([before, x, after], axis=dim)]
    unnamed x22 -> x4, local copies, waits for them, and re-layouts: 26.7 us -> 14.3 us
  transfers between devices with their start and end apart: 5 -> 2, of which waited for: 5 -> 0; matrix products, arithmetic and copies ran while one was open for 8% -> 14% of each run, Pallas kernels for 0% -> 17%
where the time goes in v2:
time: 222 us; the launch traced here: 221 us
  Pallas kernels  159 us (72%)
  local copies, waits for them, and re-layouts  37.4 us (17%)
  between operations  14.8 us (7%)
  other arithmetic  4.73 us (2%)
  starting transfers between devices  4.6 us (2%)
    pallas_call x1, Pallas kernels, exchange_and_gram(): pl.pallas_call(functools.partial(gram_kernel, grids, bands, atoms, 1.0 /...  47.6 us
    pallas_call x1, Pallas kernels, combine_and_return(): pl.pallas_call(functools.partial(combine_kernel, bands), out_shape=jax.Sh...  29.6 us
    pallas_call x1, Pallas kernels, inverse_factor(): pl.pallas_call(functools.partial(factor_kernel, step), out_shape=jax.Shap...  27.2 us
    pallas_call x1, Pallas kernels, dense_projectors(): pl.pallas_call(functools.partial(dense_kernel, extra), out_shape=(jax.Sha...  24.9 us
    pallas_call x1, Pallas kernels, update(): pl.pallas_call(update_kernel, out_shape=jax.ShapeDtypeStruct((blocks, hal...  18 us
    unnamed x4, local copies, waits for them, and re-layouts  14.3 us
    pallas_call x1, Pallas kernels, plane_part(): pl.pallas_call(functools.partial(plane_kernel, half), out_shape=jax.Shape...  12.1 us
    reshape x1, local copies, waits for them, and re-layouts, body(): cubes.reshape(2 * atom_slots, each, edge, edge, edge)  6.15 us
  transfers between devices with their start and end apart: 2, of which 0 were waited for; matrix products, arithmetic and copies ran while one was open for 14% of the time, Pallas kernels for 17%

profile of v2, /device:TPU:0, one launch (start us, length us, event | category | flops | bytes accessed | tf_op | source)
XLA Modules:
  0.0 221.1 jit_solution(14866140419473819342)
XLA Ops:
  6.5 1.0 reduce_min.9
  7.5 1.6 fusion.1
  10.4 0.7 multiply_multiply_fusion
  11.1 0.1 copy.19
  11.2 0.1 reshape.189
  11.3 2.3 %conditional.1 = (f32[128,512]{1,0:T(8,128)S(1)}, f32[1,128,512]{2,1,0:T(8,128)S(1)}) conditional(s32[]{:T(128)} %convert_element_type.36, (s32[32,512]{1,0:T(8,128)}, f32[32,4,512]{2,1,0:T(4,128)}) %tuple.19, f32[32,4,512]{2,1,0:T(4,128)} %param.10), branch_computations={%region_2.4_spmd, %region_4.5_spmd} | conditional | flops 524288 | bytes 4620376 | solution.py:487
  11.3 1.0 reshape.183
  12.4 1.0 stack_reshape.6
  13.6 4.6 %collective-permute-start.1 = (f32[130,512]{1,0:T(8,128)S(1)}, f32[130,512]{1,0:T(8,128)S(1)}, u32[]{:S(2)}, u32[]{:S(2)}) collective-permute-start(f32[130,512]{1,0:T(8,128)S(1)} %pad_maximum_fusion.1), channel_id=1, source_target_pairs={{1,8},{0,25},{9,16},{8,1},{17,24},{16,9},{25,0},{24,17},{3,10},{2,... | collective-permute-start | bytes 798728 | tf_op jit(solution)/shard_map/ppermute | solution.py:511
  18.2 6.6 %copy.27 = f32[64,16,1024]{2,0,1:T(8,128)} copy(f32[64,16,1024]{2,1,0:T(8,128)} %param.8) | data formatting | bytes 8388608 | tf_op args[0]
  24.8 3.0 %dynamic-slice_bitcast_fusion = f32[7,64,1024]{2,1,0:T(8,128)} fusion(f32[64,16,1024]{2,0,1:T(8,128)} %copy.27, s32[]{:T(128)S(6)} %select_n.92), kind=kLoop, calls=%fused_computation.6 | loop fusion | bytes 3670020 | tf_op jit(solution)/shard_map/transpose | solution.py:512
  27.8 0.0 collective-permute-start
  27.8 12.1 %shard_map.68.base_ref = f32[8,64,1024]{2,1,0:T(8,128)} custom-call(f32[16,64,1024]{2,1,0:T(8,128)} %bitcast.35, f32[8,1024]{1,0:T(8,128)} %potential_ref.1), custom_call_target="tpu_custom_call" | custom-call | flops 1610612736 | bytes 20971520 | tf_op jit(solution)/shard_map/pallas_call | solution.py:327
  39.9 0.0 collective-permute-done.1
  39.9 6.1 %reshape.191 = f32[64,4,8,8,8]{4,3,2,1,0:T(8,128)} reshape(f32[2,128,512]{2,1,0:T(8,128)S(1)} %pad_maximum_fusion) | data formatting | bytes 1048576 | tf_op jit(solution)/shard_map/reshape | solution.py:527
  46.1 6.5 %copy.23 = f32[64,8,4,8,8]{0,4,3,2,1:T(8,128)S(1)} copy(f32[64,8,4,8,8]{4,3,1,2,0:T(8,128)} %bitcast.38) | data formatting | bytes 1048576
  52.5 2.5 %pad.14.clone = f32[64,8,4,8,32]{0,4,3,2,1:T(8,128)} pad(f32[64,8,4,8,8]{0,4,3,2,1:T(8,128)S(1)} %copy.23, f32[]{:T(128)} %constant.136.clone.1), padding=0_0x0_0x0_0x0_0x0_24 | pad | bytes 2621444 | tf_op jit(solution)/shard_map/jit(_pad)/pad | solution.py:528
  55.0 4.2 %copy.21.cubes_ref = f32[64,32,256]{2,1,0:T(8,128)} copy(f32[64,32,256]{0,2,1:T(8,128)} %bitcast.39) | data formatting | bytes 4194304 | tf_op jit(solution)/shard_map/reshape | solution.py:529
  59.2 0.1 add_clamp_fusion
  59.3 0.1 and_convert_fusion
  59.4 0.1 add_bitcast_fusion
  59.5 0.6 pad_maximum_fusion.2
  60.1 0.6 pad_add_fusion.table_ref
  60.7 24.9 %shard_map.69 = (f32[64,256]{1,0:T(8,128)}, bf16[8,256,1024]{2,1,0:T(8,128)(2,1)}, bf16[8,256,1024]{2,1,0:T(8,128)(2,1)}, bf16[7,256,1024]{2,1,0:T(8,128)(2,1)}, bf16[7,256,1024]{2,1,0:T(8,128)(2,1)}) custom-call(s32[3,64]{1,0:T(4,128)} %pad_add_fusion.table_ref, f32[64,32,256]{2,1,0:T(8,128)} %copy.21.cubes_ref, f32[16,64,1024]{2,1,0:T(8,128)} %bitcast.36), custom_call_target="tpu_custom_call" | custom-call | flops 1610612736 | bytes 25165824 | tf_op jit(solution)/shard_map/pallas_call | solution.py:405
  85.6 0.0 collective-permute-done.halo_ref
  85.6 0.0 copy-start
  85.6 1.3 copy-done
  86.8 18.0 %shard_map.70.y_ref = f32[4,8,64,256]{3,2,1,0:T(8,128)} custom-call(f32[7,64,1024]{2,1,0:T(8,128)} %copy-done, f32[8,64,1024]{2,1,0:T(8,128)} %shard_map.68.base_ref, f32[16,64,1024]{2,1,0:T(8,128)} %bitcast.37, f32[64,256]{1,0:T(8,128)} %get-tuple-element.35.sums_ref, f32[1,256]{1,0:T(1,128)} %bitcast.44, bf16[8,256,1024]{2,1,0:T(8,128)(2,1)} %get-tuple-element.36.near_hi, ...), custom_call_target="tpu_custom_call" | custom-call | tf_op jit(solution)/shard_map/pallas_call | solution.py:467
  104.8 47.6 %shard_map.71 = (f32[8,256,256]{2,1,0:T(8,128)}, f32[256,256]{1,0:T(8,128)}) custom-call(f32[4,8,64,256]{3,2,1,0:T(8,128)} %shard_map.70.y_ref), custom_call_target="tpu_custom_call" | custom-call | tf_op jit(solution)/shard_map/pallas_call | solution.py:166
  152.4 27.2 %shard_map.72.x_ref = f32[256,256]{1,0:T(8,128)} custom-call(f32[256,256]{1,0:T(8,128)} %get-tuple-element.40.s_ref), custom_call_target="tpu_custom_call" | custom-call | tf_op jit(solution)/shard_map/pallas_call | solution.py:230
  179.6 29.6 %shard_map.73 = f32[4,8,64,256]{3,2,1,0:T(8,128)} custom-call(f32[256,256]{1,0:T(8,128)} %shard_map.72.x_ref, f32[8,256,256]{2,1,0:T(8,128)} %get-tuple-element.41.yq_ref), custom_call_target="tpu_custom_call" | custom-call | tf_op jit(solution)/shard_map/pallas_call | solution.py:273
  209.2 2.9 %copy.22 = f32[64,8,4,256]{3,2,1,0:T(4,128)S(1)} copy(f32[64,8,4,256]{3,0,1,2:T(8,128)} %bitcast.41) | data formatting | bytes 4194304 | tf_op jit(solution)/shard_map/transpose | solution.py:538
  212.2 2.1 reshape.193
  (11 shorter events, 0.1 us)
Async XLA Ops:
  13.6 26.3 %collective-permute-start.1 = (f32[130,512]{1,0:T(8,128)S(1)}, f32[130,512]{1,0:T(8,128)S(1)}, u32[]{:S(2)}, u32[]{:S(2)}) collective-permute-start(f32[130,512]{1,0:T(8,128)S(1)} %pad_maximum_fusion.1), channel_id=1, source_target_pairs={{1,8},{0,25},{9,16},{8,1},{17,24},{16,9},{25,0},{24,17},{3,10},{2,... | collective-permute-start | bytes 798728 | tf_op jit(solution)/shard_map/ppermute | solution.py:511
  27.8 57.8 %collective-permute-start = (f32[7,64,1024]{2,1,0:T(8,128)}, f32[7,64,1024]{2,1,0:T(8,128)S(1)}, u32[]{:S(2)}, u32[]{:S(2)}) collective-permute-start(f32[7,64,1024]{2,1,0:T(8,128)} %dynamic-slice_bitcast_fusion), channel_id=1, source_target_pairs={{1,8},{0,25},{9,16},{8,1},{17,24},{16,9},{25,0},{24,17},{3,10},{2,... | collective-permute-start | bytes 5505032 | tf_op jit(solution)/shard_map/ppermute | solution.py:513
  85.6 1.3 copy-start

commit v3 on v2

--- a/solution.py
+++ b/solution.py
@@ -46,14 +46,39 @@
 
 
 def gram_kernel(
-    grids, bands, atoms, scale, y_ref, yq_ref, s_ref, part, inbox, zbox, mine, a_sem, p_sem, z_sem, g_sem
+    grids, bands, atoms, scale, halo_ref, base_ref, rows_ref, sums_ref, scale_ref, near_hi_ref,
+    near_lo_ref, rim_hi_ref, rim_lo_ref, yq_ref, s_ref, window, near_hi, near_lo, rim_hi, rim_lo,
+    y_ref, part, inbox, zbox, mine, d_sem, n_sem, a_sem, p_sem, z_sem, g_sem,
 ):
     g, b, c = lax.axis_index("grid"), lax.axis_index("band"), lax.axis_index("atom")
     plane = bands * atoms
     me = b * atoms + c
-    rows, nb = y_ref.shape[1], y_ref.shape[2]
+    half, nb, width = y_ref.shape[1:]
     size = s_ref.shape[0]
-    depth = size // plane
+    share = size // plane
+    extra, depth = rim_hi.shape[0], window.shape[0] - rim_hi.shape[0]
+
+    loads = [
+        pltpu.make_async_copy(rim_hi_ref, rim_hi, d_sem.at[0]),
+        pltpu.make_async_copy(rim_lo_ref, rim_lo, d_sem.at[1]),
+        pltpu.make_async_copy(halo_ref, window.at[pl.ds(depth * c, extra)], d_sem.at[2]),
+        pltpu.make_async_copy(rows_ref, window.at[pl.ds(extra * (1 - c), depth)], d_sem.at[3]),
+    ]
+    for load in loads:
+        load.start()
+
+    def near_loads(k):
+        return (
+            pltpu.make_async_copy(near_hi_ref.at[k], near_hi.at[k], n_sem.at[0, k]),
+            pltpu.make_async_copy(near_lo_ref.at[k], near_lo.at[k], n_sem.at[1, k]),
+        )
+
+    def start_near(k, carry):
+        for load in near_loads(k):
+            load.start()
+        return carry
+
+    lax.fori_loop(0, half, start_near, 0)
 
     def plane_peer(k):
         p = lax.rem(me + k, plane)
@@ -67,36 +92,63 @@
             barrier, inc=1, device_id=device(lax.rem(g + k, grids), b, c), device_id_type=MESH
         )
     pl.semaphore_wait(barrier, plane - 1 + grids - 1)
-
+    for load in loads:
+        load.wait()
+
+    def gather(k, total):
+        hi, lo = split(window[depth * c + k])
+        dims = ((1,), (1,))
+        return total + mm(hi, rim_hi[k], dims) + mm(lo, rim_hi[k], dims) + mm(hi, rim_lo[k], dims)
+
+    total = lax.fori_loop(0, extra, gather, sums_ref[...])
+    hi, lo = split(total * scale_ref[...])
+    first = extra + (half - extra) * c
     own = pl.ds(pl.multiple_of(b * nb, nb), nb)
-    copies = []
-    for k in sorted(range(1, bands), key=lambda v: -v):
-        p = lax.rem(b + k, bands)
-        copies.append(
-            pltpu.make_async_remote_copy(
-                src_ref=y_ref.at[p],
-                dst_ref=yq_ref.at[:, own, :],
-                send_sem=a_sem.at[0, k - 1],
-                recv_sem=a_sem.at[1, k - 1],
-                device_id=device(g, p, c),
-                device_id_type=MESH,
+
+    def row_copies(r):
+        copies = []
+        for k in sorted(range(1, bands), key=lambda v: -v):
+            p = lax.rem(b + k, bands)
+            copies.append(
+                pltpu.make_async_remote_copy(
+                    src_ref=y_ref.at[p, r],
+                    dst_ref=yq_ref.at[r, own, :],
+                    send_sem=a_sem.at[0, r, k - 1],
+                    recv_sem=a_sem.at[1, r, k - 1],
+                    device_id=device(g, p, c),
+                    device_id_type=MESH,
+                )
             )
-        )
-        copies[-1].start()
-    yq_ref[:, own, :] = y_ref[b]
-    for copy in copies:
-        copy.wait()
-
+        return copies
+
+    def one(k, carry):
+        for load in near_loads(k):
+            load.wait()
+        nonlocal_row = mm(hi, near_hi[k]) + mm(lo, near_hi[k]) + mm(hi, near_lo[k])
+        row = base_ref[k] - STEP_SIZE * nonlocal_row
+        for d in range(1, 7):
+            pair = window[first + k + d] + window[first + k - d]
+            row = row - (STEP_SIZE * KINETIC * STENCIL[d]) * pair
+        for t in range(bands):
+            y_ref[t, k] = row[:, t * width : (t + 1) * width]
+        for copy in row_copies(k):
+            copy.start()
+        yq_ref[k, own, :] = y_ref[b, k]
+        return carry
+
+    lax.fori_loop(0, half, one, 0)
     s_ref[...] = jnp.zeros_like(s_ref)
 
     def add(r, carry):
+        for copy in row_copies(r):
+            copy.wait()
         hi, lo = split(yq_ref[r])
         cross = mm(hi, lo, ((1,), (1,)))
         s_ref[...] += mm(hi, hi, ((1,), (1,))) + (cross + cross.T)
         return carry
 
-    lax.fori_loop(0, rows, add, 0)
-    part[...] = (s_ref[...] * scale).reshape(plane, depth, size)
+    lax.fori_loop(0, half, add, 0)
+    part[...] = (s_ref[...] * scale).reshape(plane, share, size)
 
     copies = []
     for k in range(1, plane):
@@ -137,7 +189,7 @@
     total = zbox[0]
     for k in range(1, grids):
         total = total + zbox[k]
-    piece = pl.ds(pl.multiple_of(me * depth, depth), depth)
+    piece = pl.ds(pl.multiple_of(me * share, share), share)
     mine[...] = total
     copies = []
     for k in range(1, plane):
@@ -157,34 +209,45 @@
         copy.wait()
 
 
-def exchange_and_gram(y4, grids, bands, atoms, cells):
-    blocks, rows, nb, width = y4.shape
-    size = bands * nb
+def update_and_gram(halo, base, rows, sums, scale, dense, grids, bands, atoms, cells_total):
+    extra, nb, cells = halo.shape
+    half, depth = base.shape[0], rows.shape[0]
+    projectors = sums.shape[1]
+    size, width = bands * nb, cells // bands
     plane = bands * atoms
-    depth = size // plane
+    share = size // plane
     vmem = pl.BlockSpec(memory_space=pltpu.VMEM)
+    anywhere = pl.BlockSpec(memory_space=pl.ANY)
     return pl.pallas_call(
-        functools.partial(gram_kernel, grids, bands, atoms, 1.0 / cells),
+        functools.partial(gram_kernel, grids, bands, atoms, 1.0 / cells_total),
         out_shape=(
-            jax.ShapeDtypeStruct((rows, size, width), jnp.float32),
+            jax.ShapeDtypeStruct((half, size, width), jnp.float32),
             jax.ShapeDtypeStruct((size, size), jnp.float32),
         ),
-        in_specs=[vmem],
+        in_specs=[anywhere, vmem, anywhere, vmem, vmem] + [anywhere] * 4,
         out_specs=(vmem, vmem),
         scratch_shapes=[
-            pltpu.VMEM((plane, depth, size), jnp.float32),
-            pltpu.VMEM((plane - 1, depth, size), jnp.float32),
-            pltpu.VMEM((grids, depth, size), jnp.float32),
-            pltpu.VMEM((depth, size), jnp.float32),
-            pltpu.SemaphoreType.DMA((2, bands - 1)),
+            pltpu.VMEM((depth + extra, nb, cells), jnp.float32),
+            pltpu.VMEM((half, projectors, cells), jnp.bfloat16),
+            pltpu.VMEM((half, projectors, cells), jnp.bfloat16),
+            pltpu.VMEM((extra, projectors, cells), jnp.bfloat16),
+            pltpu.VMEM((extra, projectors, cells), jnp.bfloat16),
+            pltpu.VMEM((bands, half, nb, width), jnp.float32),
+            pltpu.VMEM((plane, share, size), jnp.float32),
+            pltpu.VMEM((plane - 1, share, size), jnp.float32),
+            pltpu.VMEM((grids, share, size), jnp.float32),
+            pltpu.VMEM((share, size), jnp.float32),
+            pltpu.SemaphoreType.DMA((4,)),
+            pltpu.SemaphoreType.DMA((2, half)),
+            pltpu.SemaphoreType.DMA((2, half, bands - 1)),
             pltpu.SemaphoreType.DMA((2, plane - 1)),
             pltpu.SemaphoreType.DMA((2, grids - 1)),
             pltpu.SemaphoreType.DMA((2, plane - 1)),
         ],
         compiler_params=pltpu.CompilerParams(
-            collective_id=0, has_side_effects=True, vmem_limit_bytes=56 << 20
+            collective_id=0, has_side_effects=True, vmem_limit_bytes=60 << 20
         ),
-    )(y4)
+    )(halo, base, rows, sums, scale, *dense)
 
 
 def factor_kernel(step, s_ref, x_ref, work):
@@ -193,35 +256,38 @@
     rows = lax.broadcasted_iota(jnp.int32, (size, size), 0)
     cols = lax.broadcasted_iota(jnp.int32, (size, size), 1)
     work[:, size:] = jnp.where(rows == cols, 1.0, 0.0)
-    row = lax.broadcasted_iota(jnp.int32, (step, 1), 0)
-    eye = jnp.where(
-        lax.broadcasted_iota(jnp.int32, (step, step), 0)
-        == lax.broadcasted_iota(jnp.int32, (step, step), 1),
-        1.0,
-        0.0,
-    )
+    lanes = 2 * step
+    row = lax.broadcasted_iota(jnp.int32, (8, lanes), 0)
+    lane = lax.broadcasted_iota(jnp.int32, (8, lanes), 1)
     for k in range(size // step):
         lo, hi = k * step, (k + 1) * step
-        pair = jnp.concatenate([work[lo:hi, lo:hi], eye], axis=1)
-        scales = jnp.zeros((step, 1), jnp.float32)
+        tiles = []
+        for t in range(step // 8):
+            eye = jnp.where(lane[:, :step] == row[:, :step] + t * 8, 1.0, 0.0)
+            tiles.append(
+                jnp.concatenate([work[lo + t * 8 : lo + t * 8 + 8, lo:hi], eye], axis=1)
+            )
+        lines = []
         for j in range(step):
-            line = pair[j : j + 1, :]
-            pivot = pair[j : j + 1, j : j + 1]
-            column = pair[:, j : j + 1]
-            scales = jnp.where(row == j, lax.rsqrt(pivot), scales)
-            ratio = jnp.where(row > j, column / pivot, 0.0)
-            pair = pair - ratio * line
-        inverse = pair[:, step:] * scales
-        block = mm6(inverse, work[lo:hi, :])
-        x_ref[lo:hi, :] = block[:, size:]
+            t, r = j // 8, j % 8
+            column = {
+                u: jnp.broadcast_to(tiles[u][:, j : j + 1], (8, lanes)) for u in range(t, step // 8)
+            }
+            scaled = tiles[t][r : r + 1, :] * lax.rsqrt(column[t][r : r + 1, :])
+            lines.append(scaled[:, step:])
+            ratio = lax.rsqrt(column[t][r : r + 1, :])
+            wide = jnp.broadcast_to(scaled * ratio, (8, lanes))
+            tiles[t] = tiles[t] - jnp.where(row > r, column[t], 0.0) * wide
+            for u in range(t + 1, step // 8):
+                tiles[u] = tiles[u] - column[u] * wide
+        inverse = jnp.concatenate(lines, axis=0)
+        right = mm3(inverse, work[lo:hi, size : size + hi])
+        x_ref[lo:hi, :hi] = right
         if hi < size:
-            work[hi:, :] = work[hi:, :] - mm6(block[:, hi:size], block, ((0,), (0,)))
-
-
-def mm6(a, b, dims=((1,), (0,))):
-    return lax.dot_general(
-        a, b, (dims, ((), ())), precision=HIGHEST, preferred_element_type=jnp.float32
-    )
+            x_ref[lo:hi, hi:] = jnp.zeros((step, size - hi), jnp.float32)
+            left = mm3(inverse, work[lo:hi, hi:size])
+            work[hi:, hi:size] = work[hi:, hi:size] - mm3(left, left, ((0,), (0,)))
+            work[hi:, size : size + hi] = work[hi:, size : size + hi] - mm3(left, right, ((0,), (0,)))
 
 
 def inverse_factor(s, step):
@@ -338,7 +404,8 @@
 
 
 def dense_kernel(
-    extra, table_ref, cubes_ref, rows_ref, sums_ref, near_hi, near_lo, rim_hi, rim_lo, dense
+    extra, edge, table_ref, own_ref, other_ref, rows_ref, sums_ref, near_hi, near_lo, rim_hi, rim_lo,
+    dense, cubes,
 ):
     core = lax.axis_index("atom")
     half, projectors, cells = near_hi.shape
@@ -346,29 +413,41 @@
     window = depth + extra
     atoms = table_ref.shape[1]
     each = projectors // atoms
-    planes = cubes_ref.shape[1] // each
+    count = own_ref.shape[0]
+    flat, wide = edge * edge, edge * CY
 
     def clear(w, carry):
-        dense[w] = jnp.zeros((projectors, cells), jnp.float32)
+        dense[w] = jnp.zeros(dense.shape[1:], jnp.float32)
         return carry
 
     lax.fori_loop(0, window, clear, 0)
+    point = lax.broadcasted_iota(jnp.int32, (flat, wide), 0)
+    place = lax.broadcasted_iota(jnp.int32, (flat, wide), 1)
+    spread = (point // edge == place // CY) & (point % edge == place % CY)
+    spread = jnp.where(spread, 1.0, 0.0).astype(jnp.bfloat16)
+    for e in range(edge):
+        for values, low in ((own_ref, 0), (other_ref, count)):
+            hi, lo = split(values[:count, e * flat : (e + 1) * flat])
+            cubes[e, low : low + count, :] = mm(hi, spread) + mm(lo, spread)
     pair = 8 // each
 
     def build(p, carry):
+        rows = pl.ds(pl.multiple_of(p * 8, 8), 8)
+        group = dense.at[:, rows, :]
         for h in range(pair):
             atom = p * pair + h
 
             @pl.when(table_ref[2, atom] > 0)
             def _():
-                cube = cubes_ref[atom]
-                rest = jnp.zeros((cube.shape[0], cells - cube.shape[1]), jnp.float32)
-                moved = pltpu.roll(jnp.concatenate([cube, rest], axis=1), table_ref[1, atom], 1)
+                lane = table_ref[1, atom]
                 start = table_ref[0, atom]
-                group = dense.at[:, pl.ds(pl.multiple_of(p * 8, 8), 8), :]
-                for e in range(planes):
-                    group[start + e, h * each : (h + 1) * each, :] = moved[
-                        e * each : (e + 1) * each, :
+                cube = cubes[:, rows, :].reshape(edge * 8, wide)
+                cube = jnp.concatenate([cube, jnp.zeros((edge * 8, 128), jnp.float32)], axis=1)
+                moved = pltpu.roll(cube, lax.rem(lane, 128), 1).reshape(edge, 8, wide + 128)
+                at = pl.ds(pl.multiple_of(lane // 128 * 128, 128), wide + 128)
+                for e in range(edge):
+                    group[start + e, h * each : (h + 1) * each, at] = moved[
+                        e, h * each : (h + 1) * each, :
                     ]
 
         return carry
@@ -378,100 +457,46 @@
     sums_ref[...] = jnp.zeros_like(sums_ref)
 
     def gather(r, carry):
-        sums_ref[...] += mm3(rows_ref[r], dense[r + ahead], ((1,), (1,)))
+        sums_ref[...] += mm3(rows_ref[r], dense[r + ahead, :, :cells], ((1,), (1,)))
         return carry
 
     lax.fori_loop(0, depth, gather, 0)
     own = extra + (half - extra) * core
 
     def keep_near(k, carry):
-        near_hi[k], near_lo[k] = split(dense[own + k])
+        near_hi[k], near_lo[k] = split(dense[own + k, :, :cells])
         return carry
 
     def keep_rim(k, carry):
-        rim_hi[k], rim_lo[k] = split(dense[depth * core + k])
+        rim_hi[k], rim_lo[k] = split(dense[depth * core + k, :, :cells])
         return carry
 
     lax.fori_loop(0, half, keep_near, 0)
     lax.fori_loop(0, extra, keep_rim, 0)
 
 
-def dense_projectors(table, cubes, rows, half, extra, each):
+def dense_projectors(table, ordered, other, rows, half, extra, each, edge):
     depth, nb, cells = rows.shape
     projectors = table.shape[1] * each
     vmem = pl.BlockSpec(memory_space=pltpu.VMEM)
     near = jax.ShapeDtypeStruct((half, projectors, cells), jnp.bfloat16)
     rim = jax.ShapeDtypeStruct((extra, projectors, cells), jnp.bfloat16)
     return pl.pallas_call(
-        functools.partial(dense_kernel, extra),
+        functools.partial(dense_kernel, extra, edge),
         out_shape=(jax.ShapeDtypeStruct((nb, projectors), jnp.float32), near, near, rim, rim),
-        in_specs=[pl.BlockSpec(memory_space=pltpu.SMEM), vmem, vmem],
+        in_specs=[pl.BlockSpec(memory_space=pltpu.SMEM), vmem, vmem, vmem],
         out_specs=(vmem,) * 5,
-        scratch_shapes=[pltpu.VMEM((depth + extra, projectors, cells), jnp.float32)],
+        scratch_shapes=[
+            pltpu.VMEM((depth + extra, projectors, cells + 128), jnp.float32),
+            pltpu.VMEM((edge, projectors, edge * CY), jnp.float32),
+        ],
         compiler_params=pltpu.CompilerParams(vmem_limit_bytes=60 << 20),
         cost_estimate=pl.CostEstimate(
             flops=6 * depth * nb * cells * projectors,
             bytes_accessed=4 * (depth + half) * projectors * cells,
             transcendentals=0,
         ),
-    )(table, cubes, rows)
-
-
-def update_kernel(
-    halo_ref, base_ref, rows_ref, sums_ref, scale_ref, near_hi, near_lo, rim_hi, rim_lo, y_ref, window
-):
-    core = lax.axis_index("atom")
-    extra, nb, cells = halo_ref.shape
-    depth = rows_ref.shape[0]
-    half = base_ref.shape[0]
-    blocks, width = y_ref.shape[0], y_ref.shape[3]
-    ahead = extra * (1 - core)
-
-    def put_rows(r, carry):
-        window[r + ahead] = rows_ref[r]
-        return carry
-
-    def put_halo(k, carry):
-        window[depth * core + k] = halo_ref[k]
-        return carry
-
-    lax.fori_loop(0, depth, put_rows, 0)
-    lax.fori_loop(0, extra, put_halo, 0)
-
-    def gather(k, total):
-        hi, lo = split(halo_ref[k])
-        dims = ((1,), (1,))
-        return total + mm(hi, rim_hi[k], dims) + mm(lo, rim_hi[k], dims) + mm(hi, rim_lo[k], dims)
-
-    total = lax.fori_loop(0, extra, gather, sums_ref[...])
-    hi, lo = split(total * scale_ref[...])
-    own = extra + (half - extra) * core
-
-    def one(k, carry):
-        nonlocal_row = mm(hi, near_hi[k]) + mm(lo, near_hi[k]) + mm(hi, near_lo[k])
-        row = base_ref[k] - STEP_SIZE * nonlocal_row
-        for d in range(1, 7):
-            pair = window[own + k + d] + window[own + k - d]
-            row = row - (STEP_SIZE * KINETIC * STENCIL[d]) * pair
-        for b in range(blocks):
-            y_ref[b, k] = row[:, b * width : (b + 1) * width]
-        return carry
-
-    lax.fori_loop(0, half, one, 0)
-
-
-def update(halo, base, rows, sums, scale, near_hi, near_lo, rim_hi, rim_lo, blocks):
-    extra, nb, cells = halo.shape
-    half, depth = base.shape[0], rows.shape[0]
-    vmem = pl.BlockSpec(memory_space=pltpu.VMEM)
-    return pl.pallas_call(
-        update_kernel,
-        out_shape=jax.ShapeDtypeStruct((blocks, half, nb, cells // blocks), jnp.float32),
-        in_specs=[vmem] * 9,
-        out_specs=vmem,
-        scratch_shapes=[pltpu.VMEM((depth + extra, nb, cells), jnp.float32)],
-        compiler_params=pltpu.CompilerParams(vmem_limit_bytes=56 << 20),
-    )(halo, base, rows, sums, scale, near_hi, near_lo, rim_hi, rim_lo)
+    )(table, ordered, other, rows)
 
 
 def in_cube_order(projectors, sphere_index, edge, plane_cells):
@@ -500,6 +525,11 @@
         route.append((i * groups + 1, (i + 1) % grids * groups))
         route.append((i * groups, (i - 1) % grids * groups + 1))
 
+    edge_rows = lax.dynamic_slice_in_dim(psi, core * (depth - extra), extra, 1).transpose(1, 0, 2)
+    edge_rows, psi, projectors, sphere_index = lax.optimization_barrier(
+        (edge_rows, psi, projectors, sphere_index)
+    )
+    halo = lax.ppermute(edge_rows, ("grid", "atom"), route)
     ordered, first = in_cube_order(projectors, sphere_index, edge, plane_cells)
     alive_mask = (lax.iota(jnp.int32, atom_slots) < atom_count[0]).astype(jnp.float32)
     scaled = strength * alive_mask[:, None] / math.sqrt(points)
@@ -509,9 +539,6 @@
     first_line = jnp.pad(first.astype(jnp.float32), (0, points - atom_slots))[None]
     sent = jnp.concatenate([ordered.reshape(count, points), scaled_line, first_line], axis=0)
     got = lax.ppermute(sent, ("grid", "atom"), route)
-    edge_rows = lax.dynamic_slice_in_dim(psi, core * (depth - extra), extra, 1).transpose(1, 0, 2)
-    halo = lax.ppermute(edge_rows, ("grid", "atom"), route)
-
     rows = psi.transpose(1, 0, 2)
     base = plane_part(rows, potential)
     other_first = got[-1, :atom_slots].astype(jnp.int32)
@@ -523,16 +550,13 @@
     touches = (bottom < half * (core + 1)) & (bottom + edge > half * core)
     start = jnp.clip(bottom + extra * (1 - core), 0, depth + extra - edge)
     table = jnp.stack([start, lane, touches.astype(jnp.int32)])
-    cubes = jnp.stack([ordered.reshape(count, points), got[:count]])
-    cubes = cubes.reshape(2 * atom_slots, each, edge, edge, edge).transpose(0, 2, 1, 3, 4)
-    cubes = jnp.pad(cubes, ((0, 0), (0, 0), (0, 0), (0, 0), (0, CY - edge)))
-    cubes = cubes.reshape(2 * atom_slots, edge * each, edge * CY)
-    dense = dense_projectors(table, cubes, rows, half, extra, each)
+    flat = ordered.reshape(count, points)
+    dense = dense_projectors(table, flat, got, rows, half, extra, each, edge)
     scale = jnp.concatenate([scaled.reshape(-1), other_scaled])[None]
-    y4 = update(halo, base, rows, dense[0], scale, *dense[1:], bands)
-
     cells_total = grids * depth * plane_cells
-    gathered, intersection_matrix = exchange_and_gram(y4, grids, bands, groups, cells_total)
+    gathered, intersection_matrix = update_and_gram(
+        halo, base, rows, dense[0], scale, dense[1:], grids, bands, groups, cells_total
+    )
     inverse = inverse_factor(intersection_matrix, band_rows)
     pieces = combine_and_return(inverse, gathered, bands)
     return pieces.transpose(2, 1, 0, 3).reshape(band_rows, half, plane_cells)

time: 222 us -> 210 us (0.946)
  waiting for transfers between devices: 0.01 us -> 21.5 us
  local copies, waits for them, and re-layouts: 37.4 us -> 18.1 us
  Pallas kernels: 159 us -> 147 us
    ppermute x1, waiting for transfers between devices: 0.01 us -> 21.5 us  [body(): got = lax.ppermute(sent, ('grid', 'atom'), route)]
    pallas_call x3 -> x2, Pallas kernels: 90.4 us -> 79.4 us  [the longest x1 53.5 us: update_and_gram(): pl.pallas_call(functools.partial(gram_kernel, grids, bands, atoms, 1.0 /...]
    unnamed x4 -> x7, local copies, waits for them, and re-layouts: 14.3 us -> 3.58 us
    reshape x2 -> x0, local copies, waits for them, and re-layouts: 10.3 us -> none  [the longest x1 6.15 us: body(): cubes.reshape(2 * atom_slots, each, edge, edge, edge)]
    optimization_barrier x0 -> x1, local copies, waits for them, and re-layouts: none -> 6.56 us  [body(): lax.optimization_barrier((edge_rows, psi, projectors, sphere_index))]
    ppermute x1, starting transfers between devices: 4.58 us -> 0.07 us  [body(): got = lax.ppermute(sent, ('grid', 'atom'), route)]
    ppermute x1, starting transfers between devices: 0.02 us -> 3.93 us  [body(): halo = lax.ppermute(edge_rows, ('grid', 'atom'), route)]
    transpose x1 -> x0, local copies, waits for them, and re-layouts: 2.98 us -> none  [body(): lax.dynamic_slice_in_dim(psi, core * (depth - extra), extra, 1)]
  transfers between devices with their start and end apart: 2 -> 2, of which waited for: 0 -> 1; matrix products, arithmetic and copies ran while one was open for 14% -> 6% of each run, Pallas kernels for 17% -> 18%
where the time goes in v3:
time: 210 us
  Pallas kernels  147 us (70%)
  waiting for transfers between devices  21.5 us (10%)
  local copies, waits for them, and re-layouts  18.1 us (9%)
  between operations  14.8 us (7%)
  other arithmetic  4.7 us (2%)
  starting transfers between devices  4 us (2%)
    pallas_call x1, Pallas kernels, update_and_gram(): pl.pallas_call(functools.partial(gram_kernel, grids, bands, atoms, 1.0 /...  53.5 us
    pallas_call x1, Pallas kernels, combine_and_return(): pl.pallas_call(functools.partial(combine_kernel, bands), out_shape=jax.Sh...  30 us
    pallas_call x1, Pallas kernels, dense_projectors(): pl.pallas_call(functools.partial(dense_kernel, extra, edge), out_shape=(j...  26 us
    pallas_call x1, Pallas kernels, inverse_factor(): pl.pallas_call(functools.partial(factor_kernel, step), out_shape=jax.Shap...  25.3 us
    ppermute x1, waiting for transfers between devices, body(): got = lax.ppermute(sent, ('grid', 'atom'), route)  21.5 us
    pallas_call x1, Pallas kernels, plane_part(): pl.pallas_call(functools.partial(plane_kernel, half), out_shape=jax.Shape...  12.3 us
    optimization_barrier x1, local copies, waits for them, and re-layouts, body(): lax.optimization_barrier((edge_rows, psi, projectors, sphere_index))  6.56 us
  transfers between devices with their start and end apart: 2, of which 1 were waited for; matrix products, arithmetic and copies ran while one was open for 6% of the time, Pallas kernels for 18%

profile of v3, /device:TPU:0, one launch (start us, length us, event | category | flops | bytes accessed | tf_op | source)
XLA Modules:
  0.0 210.1 jit_solution(15968213607456853593)
XLA Ops:
  6.5 0.0 copy-start.1
  6.5 2.7 %constant_dynamic-slice_fusion = f32[64,7,1024]{2,1,0:T(8,128)S(1)} fusion(f32[64,16,1024]{2,1,0:T(8,128)} %param.8, s32[]{:T(128)S(6)} %select_n.82), kind=kLoop, calls=%fused_computation.59 | loop fusion | bytes 3670020 | tf_op jit(solution)/shard_map/dynamic_slice | solution.py:528
  9.2 2.3 %copy.23 = f32[64,7,1024]{2,0,1:T(8,128)} copy(f32[64,7,1024]{2,1,0:T(8,128)S(1)} %constant_dynamic-slice_fusion) | data formatting | bytes 3670016
  11.5 3.9 %collective-permute-start = (f32[7,64,1024]{2,1,0:T(8,128)}, f32[7,64,1024]{2,1,0:T(8,128)S(1)}, u32[]{:S(2)}, u32[]{:S(2)}) collective-permute-start(f32[7,64,1024]{2,1,0:T(8,128)} %bitcast.29), channel_id=1, source_target_pairs={{1,8},{0,25},{9,16},{8,1},{17,24},{16,9},{25,0},{24,17},{3,10},{2,... | collective-permute-start | bytes 5505032 | tf_op jit(solution)/shard_map/ppermute | solution.py:532
  16.1 0.7 multiply_multiply_fusion
  16.8 0.1 copy.16
  16.9 0.1 reshape.163
  17.0 1.0 reduce_min.9
  18.0 1.6 fusion.1
  20.2 0.0 copy-done.1
  20.2 0.1 conditional.1
  20.2 0.1 reshape.159
  20.4 0.1 collective-permute-start.1
  20.5 6.6 %copy.22 = f32[64,16,1024]{2,0,1:T(8,128)} copy(f32[64,16,1024]{2,1,0:T(8,128)} %param.8) | data formatting | bytes 8388608 | tf_op jit(solution)/shard_map/optimization_barrier | solution.py:529
  27.0 12.3 %shard_map.64.base_ref = f32[8,64,1024]{2,1,0:T(8,128)} custom-call(f32[16,64,1024]{2,1,0:T(8,128)} %bitcast.32, f32[8,1024]{1,0:T(8,128)} %potential_ref.1), custom_call_target="tpu_custom_call" | custom-call | flops 1610612736 | bytes 20971520 | tf_op jit(solution)/shard_map/pallas_call | solution.py:393
  39.3 21.5 %collective-permute-done.1.other_ref = f32[130,512]{1,0:T(8,128)S(1)} collective-permute-done((f32[130,512]{1,0:T(8,128)S(1)}, f32[130,512]{1,0:T(8,128)S(1)}, u32[]{:S(2)}, u32[]{:S(2)}) %collective-permute-start.1) | collective-permute-done | bytes 266272 | tf_op jit(solution)/shard_map/ppermute | solution.py:541
  60.7 0.0 copy-start.2
  60.8 0.1 add_clamp_fusion
  60.8 0.1 and_convert_fusion
  60.9 0.1 add_bitcast_fusion
  61.0 0.6 pad_maximum_fusion.1
  61.6 0.6 pad_add_fusion.table_ref
  62.2 0.0 copy-done.2
  62.2 26.0 %shard_map.65 = (f32[64,256]{1,0:T(8,128)}, bf16[8,256,1024]{2,1,0:T(8,128)(2,1)}, bf16[8,256,1024]{2,1,0:T(8,128)(2,1)}, bf16[7,256,1024]{2,1,0:T(8,128)(2,1)}, bf16[7,256,1024]{2,1,0:T(8,128)(2,1)}) custom-call(s32[3,64]{1,0:T(4,128)} %pad_add_fusion.table_ref, f32[128,512]{1,0:T(8,128)S(1)} %get-tuple-element.49.own_ref, f32[130,512]{1,0:T(8,128)} %copy-done.2, ...), custom_call_target="tpu_custom_call" | custom-call | flops 1610612736 | bytes 25165824 | tf_op jit(solution)/shard_map/pallas_call | solution.py:484
  88.2 0.0 collective-permute-done.halo_ref
  88.2 0.0 copy-start
  88.2 1.3 copy-done
  89.5 53.5 %shard_map.66 = (f32[8,256,256]{2,1,0:T(8,128)}, f32[256,256]{1,0:T(8,128)}) custom-call(f32[7,64,1024]{2,1,0:T(8,128)} %copy-done, f32[8,64,1024]{2,1,0:T(8,128)} %shard_map.64.base_ref, f32[16,64,1024]{2,1,0:T(8,128)} %bitcast.34, f32[64,256]{1,0:T(8,128)} %get-tuple-element.33.sums_ref, f32[1,256]{1,0:T(1,128)} %bitcast.39, ...), custom_call_target="tpu_custom_call" | custom-call | tf_op jit(solution)/shard_map/pallas_call | solution.py:221
  142.9 25.3 %shard_map.67.x_ref = f32[256,256]{1,0:T(8,128)} custom-call(f32[256,256]{1,0:T(8,128)} %get-tuple-element.38.s_ref), custom_call_target="tpu_custom_call" | custom-call | tf_op jit(solution)/shard_map/pallas_call | solution.py:296
  168.2 30.0 %shard_map.68 = f32[4,8,64,256]{3,2,1,0:T(8,128)} custom-call(f32[256,256]{1,0:T(8,128)} %shard_map.67.x_ref, f32[8,256,256]{2,1,0:T(8,128)} %get-tuple-element.39.yq_ref), custom_call_target="tpu_custom_call" | custom-call | tf_op jit(solution)/shard_map/pallas_call | solution.py:339
  198.2 2.9 %copy.17 = f32[64,8,4,256]{3,2,1,0:T(4,128)S(1)} copy(f32[64,8,4,256]{3,0,1,2:T(8,128)} %bitcast.36) | data formatting | bytes 4194304 | tf_op jit(solution)/shard_map/transpose | solution.py:562
  201.2 2.1 reshape.165
  (9 shorter events, 0.1 us)
Async XLA Ops:
  6.5 13.7 %copy-start.1 = (f32[32,4,512]{2,1,0:T(4,128)S(1)}, f32[32,4,512]{2,1,0:T(4,128)}, u32[]{:S(2)}) copy-start(f32[32,4,512]{2,1,0:T(4,128)} %param.10) | copy-start | bytes 786436
  11.5 76.7 %collective-permute-start = (f32[7,64,1024]{2,1,0:T(8,128)}, f32[7,64,1024]{2,1,0:T(8,128)S(1)}, u32[]{:S(2)}, u32[]{:S(2)}) collective-permute-start(f32[7,64,1024]{2,1,0:T(8,128)} %bitcast.29), channel_id=1, source_target_pairs={{1,8},{0,25},{9,16},{8,1},{17,24},{16,9},{25,0},{24,17},{3,10},{2,... | collective-permute-start | bytes 5505032 | tf_op jit(solution)/shard_map/ppermute | solution.py:532
  20.4 40.4 %collective-permute-start.1 = (f32[130,512]{1,0:T(8,128)S(1)}, f32[130,512]{1,0:T(8,128)S(1)}, u32[]{:S(2)}, u32[]{:S(2)}) collective-permute-start(f32[130,512]{1,0:T(8,128)S(1)} %pad_maximum_fusion), channel_id=1, source_target_pairs={{1,8},{0,25},{9,16},{8,1},{17,24},{16,9},{25,0},{24,17},{3,10},{2,... | collective-permute-start | bytes 798728 | tf_op jit(solution)/shard_map/ppermute | solution.py:541
  60.7 1.5 copy-start.2
  88.2 1.3 copy-start

commit v4 on v3

--- a/solution.py
+++ b/solution.py
@@ -506,8 +506,11 @@
     ordered = jnp.all(sphere_index == first + offset[None])
 
     def arrange(values):
-        order = jnp.argsort(sphere_index, axis=1)
-        return jnp.take_along_axis(values, order[:, None, :], axis=2)
+        step = sphere_index - first
+        x, y = step % plane_cells // CY, step % CY
+        rank = step // plane_cells * (edge * edge) + x * edge + y
+        here = (rank[:, :, None] == lax.iota(jnp.int32, edge**3)).astype(jnp.float32)
+        return jnp.einsum("ais,aso->aio", values, here, precision=HIGHEST)
 
     return lax.cond(ordered, lambda values: values, arrange, projectors), first[:, 0]
 
@@ -525,11 +528,6 @@
         route.append((i * groups + 1, (i + 1) % grids * groups))
         route.append((i * groups, (i - 1) % grids * groups + 1))
 
-    edge_rows = lax.dynamic_slice_in_dim(psi, core * (depth - extra), extra, 1).transpose(1, 0, 2)
-    edge_rows, psi, projectors, sphere_index = lax.optimization_barrier(
-        (edge_rows, psi, projectors, sphere_index)
-    )
-    halo = lax.ppermute(edge_rows, ("grid", "atom"), route)
     ordered, first = in_cube_order(projectors, sphere_index, edge, plane_cells)
     alive_mask = (lax.iota(jnp.int32, atom_slots) < atom_count[0]).astype(jnp.float32)
     scaled = strength * alive_mask[:, None] / math.sqrt(points)
@@ -540,6 +538,9 @@
     sent = jnp.concatenate([ordered.reshape(count, points), scaled_line, first_line], axis=0)
     got = lax.ppermute(sent, ("grid", "atom"), route)
     rows = psi.transpose(1, 0, 2)
+    edge_rows = lax.dynamic_slice_in_dim(rows, core * (depth - extra), extra, 0)
+    got, edge_rows = lax.optimization_barrier((got, edge_rows))
+    halo = lax.ppermute(edge_rows, ("grid", "atom"), route)
     base = plane_part(rows, potential)
     other_first = got[-1, :atom_slots].astype(jnp.int32)
     other_scaled = got[count : count + lines].reshape(-1)[:count]

time: 210 us -> 176 us (0.84)
  waiting for transfers between devices: 21.5 us -> 3.56 us
  between operations: 14.8 us -> 1.38 us
  Pallas kernels: 147 us -> 144 us
    ppermute x1, waiting for transfers between devices: 21.5 us -> 0.01 us  [body(): got = lax.ppermute(sent, ('grid', 'atom'), route)]
    optimization_barrier x1 -> x0, local copies, waits for them, and re-layouts: 6.56 us -> none  [body(): lax.optimization_barrier((edge_rows, psi, projectors, sphere_index))]
    ppermute x1, starting transfers between devices: 0.07 us -> 4.58 us  [body(): got = lax.ppermute(sent, ('grid', 'atom'), route)]
    unnamed x7 -> x5, local copies, waits for them, and re-layouts: 3.58 us -> 7.83 us
    ppermute x1, starting transfers between devices: 3.93 us -> 0.02 us  [body(): halo = lax.ppermute(edge_rows, ('grid', 'atom'), route)]
    ppermute x1, waiting for transfers between devices: 0.01 us -> 3.56 us  [body(): halo = lax.ppermute(edge_rows, ('grid', 'atom'), route)]
    pallas_call x1, Pallas kernels: 53.5 us -> 50.8 us  [update_and_gram(): pl.pallas_call(functools.partial(gram_kernel, grids, bands, atoms, 1.0 /...]
  transfers between devices with their start and end apart: 2 -> 2, of which waited for: 1 -> 1; matrix products, arithmetic and copies ran while one was open for 6% -> 6% of each run, Pallas kernels for 18% -> 22%
where the time goes in v4:
time: 176 us; the launch traced here: 175 us
  Pallas kernels  144 us (82%)
  local copies, waits for them, and re-layouts  17.1 us (10%)
  other arithmetic  4.68 us (3%)
  starting transfers between devices  4.6 us (3%)
  waiting for transfers between devices  3.56 us (2%)
    pallas_call x1, Pallas kernels, update_and_gram(): pl.pallas_call(functools.partial(gram_kernel, grids, bands, atoms, 1.0 /...  50.8 us
    pallas_call x1, Pallas kernels, combine_and_return(): pl.pallas_call(functools.partial(combine_kernel, bands), out_shape=jax.Sh...  29.7 us
    pallas_call x1, Pallas kernels, dense_projectors(): pl.pallas_call(functools.partial(dense_kernel, extra, edge), out_shape=(j...  26 us
    pallas_call x1, Pallas kernels, inverse_factor(): pl.pallas_call(functools.partial(factor_kernel, step), out_shape=jax.Shap...  25.3 us
    pallas_call x1, Pallas kernels, plane_part(): pl.pallas_call(functools.partial(plane_kernel, half), out_shape=jax.Shape...  12.4 us
    unnamed x5, local copies, waits for them, and re-layouts  7.83 us
    ppermute x1, starting transfers between devices, body(): got = lax.ppermute(sent, ('grid', 'atom'), route)  4.58 us
    ppermute x1, waiting for transfers between devices, body(): halo = lax.ppermute(edge_rows, ('grid', 'atom'), route)  3.56 us
  transfers between devices with their start and end apart: 2, of which 1 were waited for; matrix products, arithmetic and copies ran while one was open for 6% of the time, Pallas kernels for 22%

profile of v4, /device:TPU:0, one launch (start us, length us, event | category | flops | bytes accessed | tf_op | source)
XLA Modules:
  0.0 175.5 jit_solution(9781867537703804124)
XLA Ops:
  0.7 1.0 reduce_min.9
  1.6 1.6 fusion.12
  3.9 0.7 multiply_multiply_fusion
  4.5 0.1 copy.10
  4.6 0.1 reshape.143
  4.8 1.1 conditional.1
  4.8 1.0 reshape.139
  5.9 4.6 %collective-permute-start = (f32[130,512]{1,0:T(8,128)S(1)}, f32[130,512]{1,0:T(8,128)S(1)}, u32[]{:S(2)}, u32[]{:S(2)}) collective-permute-start(f32[130,512]{1,0:T(8,128)S(1)} %pad_maximum_fusion), channel_id=1, source_target_pairs={{1,8},{0,25},{9,16},{8,1},{17,24},{16,9},{25,0},{24,17},{3,10},{2,... | collective-permute-start | bytes 798728 | tf_op jit(solution)/shard_map/ppermute | solution.py:539
  10.4 6.6 %copy.16 = f32[64,16,1024]{2,0,1:T(8,128)} copy(f32[64,16,1024]{2,1,0:T(8,128)} %param.8) | data formatting | bytes 8388608 | tf_op args[0]
  17.0 3.0 %dynamic-slice_bitcast_fusion = f32[7,64,1024]{2,1,0:T(8,128)} fusion(f32[64,16,1024]{2,0,1:T(8,128)} %copy.16, s32[]{:T(128)S(6)} %select_n.91), kind=kLoop, calls=%fused_computation.26 | loop fusion | bytes 3670020 | tf_op jit(solution)/shard_map/dynamic_slice | solution.py:541
  20.0 0.0 collective-permute-done.other_ref
  20.0 0.0 copy-start.1
  20.0 0.0 collective-permute-start.1
  20.0 12.4 %shard_map.67.base_ref = f32[8,64,1024]{2,1,0:T(8,128)} custom-call(f32[16,64,1024]{2,1,0:T(8,128)} %bitcast.22, f32[8,1024]{1,0:T(8,128)} %potential_ref.1), custom_call_target="tpu_custom_call" | custom-call | flops 1610612736 | bytes 20971520 | tf_op jit(solution)/shard_map/pallas_call | solution.py:393
  32.4 0.1 add_clamp_fusion
  32.5 0.1 and_convert_fusion
  32.5 0.1 add_bitcast_fusion
  32.6 0.6 pad_maximum_fusion.1
  33.2 0.6 pad_add_fusion.table_ref
  33.8 0.0 copy-done.1
  33.8 26.0 %shard_map.68 = (f32[64,256]{1,0:T(8,128)}, bf16[8,256,1024]{2,1,0:T(8,128)(2,1)}, bf16[8,256,1024]{2,1,0:T(8,128)(2,1)}, bf16[7,256,1024]{2,1,0:T(8,128)(2,1)}, bf16[7,256,1024]{2,1,0:T(8,128)(2,1)}) custom-call(s32[3,64]{1,0:T(4,128)} %pad_add_fusion.table_ref, f32[128,512]{1,0:T(8,128)S(1)} %get-tuple-element.44.own_ref, f32[130,512]{1,0:T(8,128)} %copy-done.1, ...), custom_call_target="tpu_custom_call" | custom-call | flops 1610612736 | bytes 25165824 | tf_op jit(solution)/shard_map/pallas_call | solution.py:484
  59.8 3.6 %collective-permute-done.1.halo_ref = f32[7,64,1024]{2,1,0:T(8,128)S(1)} collective-permute-done((f32[7,64,1024]{2,1,0:T(8,128)}, f32[7,64,1024]{2,1,0:T(8,128)S(1)}, u32[]{:S(2)}, u32[]{:S(2)}) %collective-permute-start.1) | collective-permute-done | bytes 1835040 | tf_op jit(solution)/shard_map/ppermute | solution.py:543
  63.3 0.0 copy-start
  63.4 1.3 copy-done
  64.6 50.8 %shard_map.69 = (f32[8,256,256]{2,1,0:T(8,128)}, f32[256,256]{1,0:T(8,128)}) custom-call(f32[7,64,1024]{2,1,0:T(8,128)} %copy-done, f32[8,64,1024]{2,1,0:T(8,128)} %shard_map.67.base_ref, f32[16,64,1024]{2,1,0:T(8,128)} %bitcast.24, f32[64,256]{1,0:T(8,128)} %get-tuple-element.32.sums_ref, f32[1,256]{1,0:T(1,128)} %bitcast.28, ...), custom_call_target="tpu_custom_call" | custom-call | tf_op jit(solution)/shard_map/pallas_call | solution.py:221
  115.5 25.3 %shard_map.70.x_ref = f32[256,256]{1,0:T(8,128)} custom-call(f32[256,256]{1,0:T(8,128)} %get-tuple-element.37.s_ref), custom_call_target="tpu_custom_call" | custom-call | tf_op jit(solution)/shard_map/pallas_call | solution.py:296
  140.7 29.7 %shard_map.71 = f32[4,8,64,256]{3,2,1,0:T(8,128)} custom-call(f32[256,256]{1,0:T(8,128)} %shard_map.70.x_ref, f32[8,256,256]{2,1,0:T(8,128)} %get-tuple-element.38.yq_ref), custom_call_target="tpu_custom_call" | custom-call | tf_op jit(solution)/shard_map/pallas_call | solution.py:339
  170.5 2.9 %copy.13 = f32[64,8,4,256]{3,2,1,0:T(4,128)S(1)} copy(f32[64,8,4,256]{3,0,1,2:T(8,128)} %bitcast.25) | data formatting | bytes 4194304 | tf_op jit(solution)/shard_map/transpose | solution.py:563
  173.4 2.1 %reshape.145 = f32[64,8,1024]{2,1,0:T(8,128)} reshape(f32[64,8,4,256]{3,2,1,0:T(4,128)S(1)} %copy.13) | data formatting | bytes 4194304 | tf_op jit(solution)/shard_map/reshape | solution.py:563
  (9 shorter events, 0.1 us)
Async XLA Ops:
  5.9 14.1 %collective-permute-start = (f32[130,512]{1,0:T(8,128)S(1)}, f32[130,512]{1,0:T(8,128)S(1)}, u32[]{:S(2)}, u32[]{:S(2)}) collective-permute-start(f32[130,512]{1,0:T(8,128)S(1)} %pad_maximum_fusion), channel_id=1, source_target_pairs={{1,8},{0,25},{9,16},{8,1},{17,24},{16,9},{25,0},{24,17},{3,10},{2,... | collective-permute-start | bytes 798728 | tf_op jit(solution)/shard_map/ppermute | solution.py:539
  20.0 13.8 %copy-start.1 = (f32[130,512]{1,0:T(8,128)}, f32[130,512]{1,0:T(8,128)S(1)}, u32[]{:S(2)}) copy-start(f32[130,512]{1,0:T(8,128)S(1)} %collective-permute-done.other_ref) | copy-start | bytes 798724
  20.0 43.4 %collective-permute-start.1 = (f32[7,64,1024]{2,1,0:T(8,128)}, f32[7,64,1024]{2,1,0:T(8,128)S(1)}, u32[]{:S(2)}, u32[]{:S(2)}) collective-permute-start(f32[7,64,1024]{2,1,0:T(8,128)} %dynamic-slice_bitcast_fusion), channel_id=1, source_target_pairs={{1,8},{0,25},{9,16},{8,1},{17,24},{16,9},{25,0},{24,17},{3,10},{2,... | collective-permute-start | bytes 5505032 | tf_op jit(solution)/shard_map/ppermute | solution.py:543
  63.3 1.3 copy-start
